TPU v7x, 128 devices: a whole 4x4x4 slice. The times are simulated.
128 devices in a mesh: slab: 8 (over y, core), seq: 16 (over z, x).
Axes of the slice: x: 4, y: 4, z: 4, core: 2. Of those that a mesh axis runs over, the one named last changes fastest.
Arguments:
- query: bfloat16 [32768, 3072], P(('slab', 'seq')), may hold values from -9 to 9
- key: bfloat16 [32768, 3072], P(('slab', 'seq')), may hold values from -9 to 9
- value: bfloat16 [32768, 3072], P(('slab', 'seq')), may hold values from -6 to 6
- d_out: bfloat16 [32768, 3072], P(('slab', 'seq')), may hold values from -6 to 6
- pattern: int32 [48, 256, 8], P('seq', 'slab'), may hold values from 0 to 255, as said below
Outputs:
- attended: bfloat16 [32768, 3072], P(('slab', 'seq'))
- grad_query: bfloat16 [32768, 3072], P(('slab', 'seq'))
- grad_key: bfloat16 [32768, 3072], P(('slab', 'seq'))
- grad_value: bfloat16 [32768, 3072], P(('slab', 'seq'))
Inputs may be any that keep to these rules, and one draw needn't show every extreme that they name: Every list pattern[h, b] holds 8 distinct blocks: first b itself, then blocks of b's own slab, and blocks of the adjacent slabs only (slab of block k is k // 32). A list of a slab with two neighbours holds 2 blocks of each; a list of the first or the last slab holds 2 blocks of its one neighbour. For each slab and each adjacent slab, the lists of every head together reference exactly 4 blocks of that adjacent slab, the same set for all heads.
All inputs are finite; a program needn't handle non-finite values.
Results may differ from a plain program's by a relative error of at most 0.0081.
Values may be sent and summed in bfloat16 or wider, within the bound.
A program may use at most 128 MiB of HBM per device.

v0:
```python
import functools

import jax
import jax.numpy as jnp
from jax import lax
from jax.experimental import pallas as pl
from jax.experimental.pallas import tpu as pltpu
from jax.sharding import PartitionSpec as P

CROSS = 4
HDIM = 64
BLOCK = 128
SCALE = HDIM**-0.5


def from_behind(x, axis, by):
    count = lax.axis_size(axis)
    pairs = [(i, i + by) for i in range(count) if 0 <= i + by < count]
    return lax.ppermute(x, axis, pairs)


def pack_kernel(q_ref, k_ref, v_ref, g_ref, kv_ref, qg_ref):
    for t in range(3):
        cols = slice(128 * t, 128 * t + 128)
        q, k, v, g = q_ref[:, cols], k_ref[:, cols], v_ref[:, cols], g_ref[:, cols]
        q = q * jnp.asarray(SCALE, q.dtype)
        for i in range(2):
            head = 2 * t + i
            half = slice(64 * i, 64 * i + 64)
            kv_ref[head // 3, head % 3] = jnp.concatenate([k[:, half], v[:, half]], axis=1)
            qg_ref[head // 3, head % 3] = jnp.concatenate([q[:, half], g[:, half]], axis=1)


def pack(q, k, v, g):
    rows, columns = q.shape
    spec = pl.BlockSpec((rows, 384), lambda i: (0, i))
    out = jax.ShapeDtypeStruct((16, 3, rows, 128), q.dtype)
    out_spec = pl.BlockSpec((2, 3, rows, 128), lambda i: (i, 0, 0, 0))
    return pl.pallas_call(
        pack_kernel,
        grid=(8,),
        in_specs=[spec] * 4,
        out_specs=[out_spec] * 2,
        out_shape=[out] * 2,
        cost_estimate=pl.CostEstimate(flops=0, bytes_accessed=12 << 20, transcendentals=0),
        name="pack",
    )(q, k, v, g)


def unpack_kernel(og_ref, kv_ref, o_ref, dq_ref, dk_ref, dv_ref):
    for t in range(3):
        cols = slice(128 * t, 128 * t + 128)
        a, b = 2 * t, 2 * t + 1
        og_a, og_b = og_ref[a // 3, a % 3], og_ref[b // 3, b % 3]
        kv_a, kv_b = kv_ref[a // 3, a % 3], kv_ref[b // 3, b % 3]
        dq_ref[:, cols] = jnp.concatenate([og_a[:, :64], og_b[:, :64]], axis=1)
        o_ref[:, cols] = jnp.concatenate([og_a[:, 64:], og_b[:, 64:]], axis=1)
        dk_ref[:, cols] = jnp.concatenate([kv_a[:, :64], kv_b[:, :64]], axis=1)
        dv_ref[:, cols] = jnp.concatenate([kv_a[:, 64:], kv_b[:, 64:]], axis=1)


def unpack(og, kv):
    rows = og.shape[2]
    spec = pl.BlockSpec((2, 3, rows, 128), lambda i: (i, 0, 0, 0))
    out_spec = pl.BlockSpec((rows, 384), lambda i: (0, i))
    out = jax.ShapeDtypeStruct((rows, 3072), og.dtype)
    return pl.pallas_call(
        unpack_kernel,
        grid=(8,),
        in_specs=[spec] * 2,
        out_specs=[out_spec] * 4,
        out_shape=[out] * 4,
        cost_estimate=pl.CostEstimate(flops=0, bytes_accessed=12 << 20, transcendentals=0),
        name="unpack",
    )(og, kv)


def nt(a, b):
    return lax.dot_general(a, b, (((1,), (1,)), ((), ())), preferred_element_type=jnp.float32)


def attend_kernel(
    ids_ref, kv_ref, qg_ref, prev_ref, next_ref, og_ref, dkv_ref, cross_ref, kvw, kvt, acc, sd, ex, *, blocks, per_list
):
    head = pl.program_id(0)
    bf16 = jnp.bfloat16
    own = blocks

    @pl.loop(0, own // 2)
    def _(i):
        for half in range(2):
            block = kv_ref[i, 0, half * BLOCK : half * BLOCK + BLOCK]
            kvw[2 * i + half] = block
            kvt[2 * i + half] = block.T

    for c in range(CROSS):
        kvw[own + c] = prev_ref[0, c]
        kvt[own + c] = prev_ref[0, c].T
        kvw[own + CROSS + c] = next_ref[0, c]
        kvt[own + CROSS + c] = next_ref[0, c].T
    acc[...] = jnp.zeros_like(acc)
    left = lax.broadcasted_iota(jnp.int32, (BLOCK, 128), 1) < HDIM

    @pl.loop(0, blocks)
    def _(b):
        row = pl.multiple_of((b % 2) * BLOCK, BLOCK)
        qg = qg_ref[b // 2, 0, pl.ds(row, BLOCK)]
        zero = jnp.zeros_like(qg)
        both = jnp.concatenate([jnp.where(left, qg, zero), jnp.where(left, zero, qg)], axis=0)
        base = (head * blocks + b) * per_list
        ids = [ids_ref[base + j] for j in range(per_list)]
        top = None
        for j in range(per_list):
            pair = nt(kvw[ids[j]], both)
            sd[j] = pair
            part = jnp.max(pair[:, :BLOCK].reshape(16, 8, BLOCK), axis=0)
            top = part if top is None else jnp.maximum(top, part)
        row_max = jnp.max(top, axis=0, keepdims=True)
        total = jnp.zeros((8, BLOCK), jnp.float32)
        mixed = jnp.zeros((8, BLOCK), jnp.float32)
        for j in range(per_list):
            e = jnp.exp(sd[j, :, :BLOCK] - row_max)
            sd[j, :, :BLOCK] = e
            ex[j, :, BLOCK:] = e.astype(bf16)
            total += jnp.sum(e.reshape(16, 8, BLOCK), axis=0)
            mixed += jnp.sum((e * sd[j, :, BLOCK:]).reshape(16, 8, BLOCK), axis=0)
        inverse = 1.0 / jnp.sum(total, axis=0, keepdims=True)
        correction = jnp.sum(mixed, axis=0, keepdims=True) * inverse
        for j in range(per_list):
            ex[j, :, :BLOCK] = (sd[j, :, :BLOCK] * (sd[j, :, BLOCK:] - correction)).astype(bf16)
        out = jnp.zeros((128, 2 * BLOCK), jnp.float32)
        for j in range(0, per_list, 2):
            lhs = jnp.concatenate([kvt[ids[j]], kvt[ids[j + 1]]], axis=1)
            rhs = ex[j : j + 2].reshape(2 * BLOCK, 2 * BLOCK)
            out += jnp.dot(lhs, rhs, preferred_element_type=jnp.float32)
        outs = jnp.concatenate([out[:HDIM, :BLOCK] * (inverse * SCALE), out[HDIM:, BLOCK:] * inverse], axis=0)
        og_ref[b // 2, 0, pl.ds(row, BLOCK)] = outs.T.astype(bf16)
        column = jnp.broadcast_to(inverse, (BLOCK, BLOCK)).T
        scaled = (both.astype(jnp.float32) * jnp.concatenate([column, column], axis=0)).astype(bf16)
        for j in range(per_list):
            acc[ids[j]] += jnp.dot(ex[j], scaled, preferred_element_type=jnp.float32)

    @pl.loop(0, own // 2)
    def _(i):
        for half in range(2):
            dkv_ref[i, 0, half * BLOCK : half * BLOCK + BLOCK] = acc[2 * i + half].astype(bf16)

    for c in range(2 * CROSS):
        cross_ref[0, c] = acc[own + c].astype(bf16)


def attend(ids, kv, qg, prev, nxt):
    heads, blocks, per_list = ids.shape
    rows = kv.shape[2]
    whole = pl.BlockSpec((16, 1, rows, 128), lambda h, *_: (0, h, 0, 0))
    side = pl.BlockSpec((1, CROSS, BLOCK, 128), lambda h, *_: (h, 0, 0, 0))
    window = blocks + 2 * CROSS
    f32, bf16 = jnp.float32, jnp.bfloat16
    return pl.pallas_call(
        functools.partial(attend_kernel, blocks=blocks, per_list=per_list),
        grid_spec=pltpu.PrefetchScalarGridSpec(
            num_scalar_prefetch=1,
            grid=(heads,),
            in_specs=[whole, whole, side, side],
            out_specs=[whole, whole, pl.BlockSpec((1, 2 * CROSS, BLOCK, 128), lambda h, *_: (h, 0, 0, 0))],
            scratch_shapes=[
                pltpu.VMEM((window, BLOCK, 128), bf16),
                pltpu.VMEM((window, 128, BLOCK), bf16),
                pltpu.VMEM((window, BLOCK, 128), f32),
                pltpu.VMEM((per_list, BLOCK, 2 * BLOCK), f32),
                pltpu.VMEM((per_list, BLOCK, 2 * BLOCK), bf16),
            ],
        ),
        out_shape=[
            jax.ShapeDtypeStruct((16, heads, rows, 128), bf16),
            jax.ShapeDtypeStruct((16, heads, rows, 128), bf16),
            jax.ShapeDtypeStruct((heads, 2 * CROSS, BLOCK, 128), bf16),
        ],
        compiler_params=pltpu.CompilerParams(vmem_limit_bytes=56 << 20),
        name="attend",
    )(ids.reshape(-1), kv, qg, prev, nxt)


def fix_kernel(asked_ref, dkv_ref, back_ref, out_ref):
    out_ref[...] = dkv_ref[...]
    for c in range(2 * CROSS):
        block = asked_ref[c]
        row = pl.multiple_of((block % 2) * BLOCK, BLOCK)
        here = (block // 2, 0, pl.ds(row, BLOCK))
        term = out_ref[here].astype(jnp.float32) + back_ref[0, c].astype(jnp.float32)
        out_ref[here] = term.astype(out_ref.dtype)


def fix(asked, dkv, back):
    heads, rows = dkv.shape[1:3]
    whole = pl.BlockSpec((16, 1, rows, 128), lambda h, *_: (0, h, 0, 0))
    return pl.pallas_call(
        fix_kernel,
        grid_spec=pltpu.PrefetchScalarGridSpec(
            num_scalar_prefetch=1,
            grid=(heads,),
            in_specs=[whole, pl.BlockSpec((1, 2 * CROSS, BLOCK, 128), lambda h, *_: (h, 0, 0, 0))],
            out_specs=whole,
        ),
        out_shape=jax.ShapeDtypeStruct(dkv.shape, dkv.dtype),
        name="fix",
    )(asked, dkv, back)


def first_hits(pattern, base, blocks):
    ids = jnp.arange(blocks, dtype=jnp.int32)
    hits = jnp.any(pattern.reshape(-1)[:, None] == (base + ids)[None, :], axis=0)
    rank = jnp.sum(jnp.where(ids[None, :] <= ids[:, None], hits[None, :].astype(jnp.int32), 0), axis=1)
    slots = jnp.arange(CROSS, dtype=jnp.int32)
    chosen = hits[None, :] & (rank[None, :] == slots[:, None] + 1)
    return jnp.sum(jnp.where(chosen, ids[None, :], 0), axis=1)


def local(query, key, value, d_out, pattern):
    heads, blocks, per_list = pattern.shape
    own_base = lax.axis_index("slab") * blocks
    need_prev = first_hits(pattern, own_base - blocks, blocks)
    need_next = first_hits(pattern, own_base + blocks, blocks)
    asked_next = from_behind(need_prev, "slab", -1)
    asked_prev = from_behind(need_next, "slab", 1)
    kv, qg = pack(query, key, value, d_out)
    kv = lax.all_to_all(kv, "seq", split_axis=0, concat_axis=0, tiled=True)
    qg = lax.all_to_all(qg, "seq", split_axis=0, concat_axis=0, tiled=True)
    slots = jnp.arange(CROSS, dtype=jnp.int32)
    pos_prev = jnp.sum(jnp.where(pattern[..., None] == own_base - blocks + need_prev, slots, 0), axis=-1)
    pos_next = jnp.sum(jnp.where(pattern[..., None] == own_base + blocks + need_next, slots, 0), axis=-1)
    relative = pattern - own_base
    ids = jnp.where(relative < 0, blocks + pos_prev, jnp.where(relative < blocks, relative, blocks + CROSS + pos_next))

    def taken(asked):
        return jnp.stack(
            [
                lax.dynamic_slice(kv, (asked[c] // 2, 0, (asked[c] % 2) * BLOCK, 0), (1, heads, BLOCK, 128))[0]
                for c in range(CROSS)
            ],
            axis=1,
        )

    prev = from_behind(taken(asked_next), "slab", 1)
    nxt = from_behind(taken(asked_prev), "slab", -1)
    og, dkv, cross = attend(ids, kv, qg, prev, nxt)
    og = lax.all_to_all(og, "seq", split_axis=0, concat_axis=0, tiled=True)
    back_later = from_behind(cross[:, :CROSS], "slab", -1)
    back_earlier = from_behind(cross[:, CROSS:], "slab", 1)
    dkv = fix(jnp.concatenate([asked_next, asked_prev]), dkv, jnp.concatenate([back_later, back_earlier], axis=1))
    dkv = lax.all_to_all(dkv, "seq", split_axis=0, concat_axis=0, tiled=True)
    return tuple(unpack(og, dkv))


def solution(mesh):
    rows = P(("slab", "seq"), None)
    return jax.shard_map(
        local,
        mesh=mesh,
        in_specs=(rows, rows, rows, rows, P("seq", "slab", None)),
        out_specs=(rows, rows, rows, rows),
        check_vma=False,
    )
```

profile of v0, /device:TPU:0, one launch (start us, length us, event | category | flops | bytes accessed | tf_op | source)
XLA Modules:
  0.0 305.3 jit_solution(2290257871682339568)
XLA Ops:
  0.6 8.8 %pack.1 = (bf16[16,3,256,128]{3,2,1,0:T(8,128)(2,1)}, bf16[16,3,256,128]{3,2,1,0:T(8,128)(2,1)}) custom-call(bf16[256,3072]{1,0:T(8,128)(2,1)} %q_ref.1, bf16[256,3072]{1,0:T(8,128)(2,1)} %k_ref.1, bf16[256,3072]{1,0:T(8,128)(2,1)} %v_ref.1, bf16[256,3072]{1,0:T(8,128)(2,1)} %g_ref.1), custom_call_target="tpu_custom_call" | custom-call | bytes 12582912 | tf_op jit(solution)/shard_map/pack/pallas_call | solution.py:39
  9.5 47.6 %all_to_all.20.kv_ref = bf16[16,3,256,128]{3,2,1,0:T(8,128)(2,1)S(1)} all-to-all(bf16[16,3,256,128]{3,2,1,0:T(8,128)(2,1)} %get-tuple-element.9), channel_id=1, replica_groups=mesh['slab'=8,'seq'=16] {'seq'}, dimensions={0} | all-to-all | bytes 6291456 | tf_op jit(solution)/shard_map/all_to_all | solution.py:227
  57.1 0.0 copy-start
  57.1 4.6 %all-to-all-start.1 = ((bf16[16,3,256,128]{3,2,1,0:T(8,128)(2,1)}), bf16[16,3,256,128]{3,2,1,0:T(8,128)(2,1)}, u32[]{:S(2)}, u32[]{:S(2)}) async-start(bf16[16,3,256,128]{3,2,1,0:T(8,128)(2,1)} %get-tuple-element.10), calls=%async_computation.1 | async-start | bytes 6291456 | tf_op jit(solution)/shard_map/all_to_all | solution.py:228
  61.7 0.0 copy-done.4
  61.7 0.1 copy.13
  61.8 0.1 eq.86
  61.9 0.2 compare_reduce_fusion.1
  62.1 0.1 select_reduce_fusion.3
  62.3 0.1 select_reduce_fusion.2
  62.4 0.2 select_reduce_fusion.5
  62.6 1.3 collective-permute-start
  63.9 3.0 collective-permute-start.2
  66.9 0.0 collective-permute-done
  66.9 0.6 fusion.3
  78.0 0.0 collective-permute-done.2
  78.0 0.6 fusion.2
  89.1 0.0 copy-done
  89.1 0.1 dynamic-slice_bitcast_fusion.3
  89.2 0.1 pad_maximum_fusion.1
  89.3 3.1 %collective-permute-start.1 = (bf16[3,4,128,128]{3,2,1,0:T(8,128)(2,1)S(1)}, bf16[3,4,128,128]{3,2,1,0:T(8,128)(2,1)S(1)}, u32[]{:S(2)}, u32[]{:S(2)}) collective-permute-start(bf16[3,4,128,128]{3,2,1,0:T(8,128)(2,1)S(1)} %pad_maximum_fusion.1), channel_id=1, source_target_pairs={{0,16},{16,32},{32,48},{48,64},{64,80},{80,96},{96,112},{1,17},{17... | collective-permute-start | bytes 1179656 | tf_op jit(solution)/shard_map/ppermute | solution.py:19
  92.4 0.1 pad_maximum_fusion.2
  92.5 1.3 collective-permute-start.3
  93.8 0.1 select_reduce_fusion.1
  93.9 0.1 copy.14
  93.9 0.7 reshape.44.ids_ref
  94.6 11.3 %all-to-all-done.1.qg_ref = bf16[16,3,256,128]{3,2,1,0:T(8,128)(2,1)} async-done(((bf16[16,3,256,128]{3,2,1,0:T(8,128)(2,1)}), bf16[16,3,256,128]{3,2,1,0:T(8,128)(2,1)}, u32[]{:S(2)}, u32[]{:S(2)}) %all-to-all-start.1) | async-done | bytes 3145760 | tf_op jit(solution)/shard_map/all_to_all | solution.py:228
  106.0 0.0 collective-permute-done.1.prev_ref
  106.0 0.0 copy-start.2
  106.0 0.0 collective-permute-done.3.next_ref
  106.0 0.7 copy-done.2
  106.7 0.0 copy-start.3
  106.7 0.7 copy-done.3
  107.5 99.1 %attend.1 = (bf16[16,3,256,128]{3,2,1,0:T(8,128)(2,1)}, bf16[16,3,256,128]{3,2,1,0:T(8,128)(2,1)}, bf16[3,8,128,128]{3,2,1,0:T(8,128)(2,1)}) custom-call(s32[768]{0:T(1024)} %reshape.44.ids_ref, bf16[16,3,256,128]{3,2,1,0:T(8,128)(2,1)} %copy-done, bf16[16,3,256,128]{3,2,1,0:T(8,128)(2,1)} %all-to-all-done.1.qg_ref, bf16[3,4,128,128]{3,2,1,0:T(8,128)(2,1)} %copy-done.2, ...), custom_call_target="tpu_custom_call" | custom-call | tf_op jit(solution)/shard_map/attend/pallas_call | solution.py:159
  206.5 3.7 %all-to-all-start.2 = ((bf16[16,3,256,128]{3,2,1,0:T(8,128)(2,1)}), bf16[16,3,256,128]{3,2,1,0:T(8,128)(2,1)S(1)}, u32[]{:S(2)}, u32[]{:S(2)}) async-start(bf16[16,3,256,128]{3,2,1,0:T(8,128)(2,1)} %get-tuple-element.11), calls=%async_computation.2 | async-start | bytes 6291456 | tf_op jit(solution)/shard_map/all_to_all | solution.py:247
  210.3 1.2 fusion.1
  211.5 1.3 collective-permute-start.4
  212.8 3.1 %collective-permute-start.5 = (bf16[3,4,128,128]{3,2,1,0:T(8,128)(2,1)S(1)}, bf16[3,4,128,128]{3,2,1,0:T(8,128)(2,1)S(1)}, u32[]{:S(2)}, u32[]{:S(2)}) collective-permute-start(bf16[3,4,128,128]{3,2,1,0:T(8,128)(2,1)S(1)} %get-tuple-element.29), channel_id=1, source_target_pairs={{0,16},{16,32},{32,48},{48,64},{64,80},{80,96},{96,112},{1,17},{17... | collective-permute-start | bytes 1179656 | tf_op jit(solution)/shard_map/ppermute | solution.py:19
  215.8 0.6 pad_add_fusion.asked_ref
  216.4 0.0 collective-permute-done.4
  216.4 0.7 collective-permute-done.5
  217.1 0.9 pad_maximum_fusion.back_ref
  218.1 5.3 %fix.1 = bf16[16,3,256,128]{3,2,1,0:T(8,128)(2,1)} custom-call(s32[8]{0:T(128)} %pad_add_fusion.asked_ref, bf16[16,3,256,128]{3,2,1,0:T(8,128)(2,1)} %get-tuple-element.12.dkv_ref, bf16[3,8,128,128]{3,2,1,0:T(8,128)(2,1)} %pad_maximum_fusion.back_ref), custom_call_target="tpu_custom_call" | custom-call | tf_op jit(solution)/shard_map/fix/pallas_call | solution.py:197
  223.4 30.9 %all-to-all-done.2.og_ref = bf16[16,3,256,128]{3,2,1,0:T(8,128)(2,1)S(1)} async-done(((bf16[16,3,256,128]{3,2,1,0:T(8,128)(2,1)}), bf16[16,3,256,128]{3,2,1,0:T(8,128)(2,1)S(1)}, u32[]{:S(2)}, u32[]{:S(2)}) %all-to-all-start.2) | async-done | bytes 3145760 | tf_op jit(solution)/shard_map/all_to_all | solution.py:247
  254.4 0.0 copy-start.1
  254.4 42.6 %all_to_all.21.kv_ref = bf16[16,3,256,128]{3,2,1,0:T(8,128)(2,1)} all-to-all(bf16[16,3,256,128]{3,2,1,0:T(8,128)(2,1)} %fix.1), channel_id=1, replica_groups=mesh['slab'=8,'seq'=16] {'seq'}, dimensions={0} | all-to-all | bytes 6291456 | tf_op jit(solution)/shard_map/all_to_all | solution.py:251
  297.0 0.0 copy-done.1
  297.0 8.3 %unpack.1 = (bf16[256,3072]{1,0:T(8,128)(2,1)}, bf16[256,3072]{1,0:T(8,128)(2,1)}, bf16[256,3072]{1,0:T(8,128)(2,1)}, bf16[256,3072]{1,0:T(8,128)(2,1)}) custom-call(bf16[16,3,256,128]{3,2,1,0:T(8,128)(2,1)} %copy-done.1, bf16[16,3,256,128]{3,2,1,0:T(8,128)(2,1)} %all_to_all.21.kv_ref), custom_call_target="tpu_custom_call" | custom-call | bytes 12582912 | tf_op jit(solution)/shard_map/unpack/pallas_call | solution.py:67
  (8 shorter events, 0.0 us)
Async XLA Ops:
  57.1 32.0 %copy-start = (bf16[16,3,256,128]{3,2,1,0:T(8,128)(2,1)}, bf16[16,3,256,128]{3,2,1,0:T(8,128)(2,1)S(1)}, u32[]{:S(2)}) copy-start(bf16[16,3,256,128]{3,2,1,0:T(8,128)(2,1)S(1)} %all_to_all.20.kv_ref) | copy-start | bytes 9437188
  57.1 4.6 %copy-start.4 = (s32[3,32,8]{1,2,0:T(8,128)S(1)}, s32[3,32,8]{1,2,0:T(8,128)}, u32[]{:S(2)}) copy-start(s32[3,32,8]{1,2,0:T(8,128)} %param.9) | copy-start | bytes 9220
  57.1 48.9 %all-to-all-start.1 = ((bf16[16,3,256,128]{3,2,1,0:T(8,128)(2,1)}), bf16[16,3,256,128]{3,2,1,0:T(8,128)(2,1)}, u32[]{:S(2)}, u32[]{:S(2)}) async-start(bf16[16,3,256,128]{3,2,1,0:T(8,128)(2,1)} %get-tuple-element.10), calls=%async_computation.1 | async-start | bytes 6291456 | tf_op jit(solution)/shard_map/all_to_all | solution.py:228
  62.6 4.4 %collective-permute-start = (s32[4]{0:T(128)S(1)}, s32[4]{0:T(128)S(1)}, u32[]{:S(2)}, u32[]{:S(2)}) collective-permute-start(s32[4]{0:T(128)S(1)} %get-tuple-element.18), channel_id=1, source_target_pairs={{16,0},{32,16},{48,32},{64,48},{80,64},{96,80},{112,96},{17,1},{33... | collective-permute-start | bytes 56 | tf_op jit(solution)/shard_map/ppermute | solution.py:19
  63.9 14.1 %collective-permute-start.2 = (s32[4]{0:T(128)S(1)}, s32[4]{0:T(128)S(1)}, u32[]{:S(2)}, u32[]{:S(2)}) collective-permute-start(s32[4]{0:T(128)S(1)} %get-tuple-element.19), channel_id=1, source_target_pairs={{0,16},{16,32},{32,48},{48,64},{64,80},{80,96},{96,112},{1,17},{17... | collective-permute-start | bytes 56 | tf_op jit(solution)/shard_map/ppermute | solution.py:19
  89.3 16.7 %collective-permute-start.1 = (bf16[3,4,128,128]{3,2,1,0:T(8,128)(2,1)S(1)}, bf16[3,4,128,128]{3,2,1,0:T(8,128)(2,1)S(1)}, u32[]{:S(2)}, u32[]{:S(2)}) collective-permute-start(bf16[3,4,128,128]{3,2,1,0:T(8,128)(2,1)S(1)} %pad_maximum_fusion.1), channel_id=1, source_target_pairs={{0,16},{16,32},{32,48},{48,64},{64,80},{80,96},{96,112},{1,17},{17... | collective-permute-start | bytes 1179656 | tf_op jit(solution)/shard_map/ppermute | solution.py:19
  92.5 13.5 %collective-permute-start.3 = (bf16[3,4,128,128]{3,2,1,0:T(8,128)(2,1)S(1)}, bf16[3,4,128,128]{3,2,1,0:T(8,128)(2,1)S(1)}, u32[]{:S(2)}, u32[]{:S(2)}) collective-permute-start(bf16[3,4,128,128]{3,2,1,0:T(8,128)(2,1)S(1)} %pad_maximum_fusion.2), channel_id=1, source_target_pairs={{16,0},{32,16},{48,32},{64,48},{80,64},{96,80},{112,96},{17,1},{33... | collective-permute-start | bytes 1179656 | tf_op jit(solution)/shard_map/ppermute | solution.py:19
  106.0 0.7 copy-start.2
  106.7 0.7 copy-start.3
  206.5 47.8 %all-to-all-start.2 = ((bf16[16,3,256,128]{3,2,1,0:T(8,128)(2,1)}), bf16[16,3,256,128]{3,2,1,0:T(8,128)(2,1)S(1)}, u32[]{:S(2)}, u32[]{:S(2)}) async-start(bf16[16,3,256,128]{3,2,1,0:T(8,128)(2,1)} %get-tuple-element.11), calls=%async_computation.2 | async-start | bytes 6291456 | tf_op jit(solution)/shard_map/all_to_all | solution.py:247
  211.5 5.0 %collective-permute-start.4 = (bf16[3,4,128,128]{3,2,1,0:T(8,128)(2,1)S(1)}, bf16[3,4,128,128]{3,2,1,0:T(8,128)(2,1)S(1)}, u32[]{:S(2)}, u32[]{:S(2)}) collective-permute-start(bf16[3,4,128,128]{3,2,1,0:T(8,128)(2,1)S(1)} %get-tuple-element.28), channel_id=1, source_target_pairs={{16,0},{32,16},{48,32},{64,48},{80,64},{96,80},{112,96},{17,1},{33... | collective-permute-start | bytes 1179656 | tf_op jit(solution)/shard_map/ppermute | solution.py:19
  212.8 4.4 %collective-permute-start.5 = (bf16[3,4,128,128]{3,2,1,0:T(8,128)(2,1)S(1)}, bf16[3,4,128,128]{3,2,1,0:T(8,128)(2,1)S(1)}, u32[]{:S(2)}, u32[]{:S(2)}) collective-permute-start(bf16[3,4,128,128]{3,2,1,0:T(8,128)(2,1)S(1)} %get-tuple-element.29), channel_id=1, source_target_pairs={{0,16},{16,32},{32,48},{48,64},{64,80},{80,96},{96,112},{1,17},{17... | collective-permute-start | bytes 1179656 | tf_op jit(solution)/shard_map/ppermute | solution.py:19
  254.4 42.6 %copy-start.1 = (bf16[16,3,256,128]{3,2,1,0:T(8,128)(2,1)}, bf16[16,3,256,128]{3,2,1,0:T(8,128)(2,1)S(1)}, u32[]{:S(2)}) copy-start(bf16[16,3,256,128]{3,2,1,0:T(8,128)(2,1)S(1)} %all-to-all-done.2.og_ref) | copy-start | bytes 9437188
where the time goes:
time: 307 us; the launch traced here: 305 us
  Pallas kernels  122 us (40%)
  blocking collectives  90.2 us (29%)
  waiting for transfers between devices  43 us (14%)
  between operations  21.8 us (7%)
  starting transfers between devices  21.4 us (7%)
  local copies, waits for them, and re-layouts  4.9 us (2%)
    pallas_call x1, Pallas kernels, attend(): pl.pallas_call(functools.partial(attend_kernel, blocks=blocks, per_list=p...  99.1 us
    all_to_all x1, blocking collectives, local(): kv = lax.all_to_all(kv, 'seq', split_axis=0, concat_axis=0, tiled=True)  47.6 us
    all_to_all x1, blocking collectives, local(): dkv = lax.all_to_all(dkv, 'seq', split_axis=0, concat_axis=0, tiled=True)  42.6 us
    all_to_all x1, waiting for transfers between devices, local(): og = lax.all_to_all(og, 'seq', split_axis=0, concat_axis=0, tiled=True)  30.9 us
    ppermute x6, starting transfers between devices, from_behind(): return lax.ppermute(x, axis, pairs)  13.1 us
    all_to_all x1, waiting for transfers between devices, local(): qg = lax.all_to_all(qg, 'seq', split_axis=0, concat_axis=0, tiled=True)  11.3 us
    pallas_call x1, Pallas kernels, pack(): pl.pallas_call(pack_kernel, grid=(8,), in_specs=[spec] * 4, out_specs=[ou...  8.84 us
    pallas_call x1, Pallas kernels, unpack(): pl.pallas_call(unpack_kernel, grid=(8,), in_specs=[spec] * 2, out_specs=[...  8.32 us
  transfers between devices with their start and end apart: 8, of which 3 were waited for; matrix products, arithmetic and copies ran while one was open for 2% of the time, Pallas kernels for 2%

commit v1 on v0

v1 whole, which is shorter than its diff:
```python
import functools

import jax
import jax.numpy as jnp
from jax import lax
from jax.experimental import pallas as pl
from jax.experimental.pallas import tpu as pltpu
from jax.sharding import PartitionSpec as P

CROSS = 4
HDIM = 64
BLOCK = 128
SCALE = HDIM**-0.5
PEERS = 16
STEP = 7
MESH = pl.DeviceIdType.MESH
SPREAD = ((0, 1), (1, 0), (0, 3), (3, 0), (1, 1), (3, 3), (1, 3), (3, 1), (0, 2), (2, 0), (1, 2), (2, 1), (3, 2), (2, 3), (2, 2))


def from_behind(x, axis, by):
    count = lax.axis_size(axis)
    pairs = [(i, i + by) for i in range(count) if 0 <= i + by < count]
    return lax.ppermute(x, axis, pairs)


def slot_of(dz, dx):
    return ((dz % 4) * 4 + dx % 4) * STEP % PEERS


def pack_kernel(q_ref, k_ref, v_ref, g_ref, kv_ref, qg_ref):
    for t in range(3):
        cols = slice(128 * t, 128 * t + 128)
        q, k, v, g = q_ref[:, cols], k_ref[:, cols], v_ref[:, cols], g_ref[:, cols]
        q = q * jnp.asarray(SCALE, q.dtype)
        for i in range(2):
            head = 2 * t + i
            half = slice(64 * i, 64 * i + 64)
            kv = jnp.concatenate([k[:, half], v[:, half]], axis=1)
            qg = jnp.concatenate([q[:, half], g[:, half]], axis=1)
            for part in range(2):
                rows = slice(BLOCK * part, BLOCK * part + BLOCK)
                kv_ref[head // 3, head % 3, part] = kv[rows]
                qg_ref[head // 3, head % 3, part] = qg[rows]


def pack(q, k, v, g):
    rows = q.shape[0]
    spec = pl.BlockSpec((rows, 384), lambda i: (0, i))
    out = jax.ShapeDtypeStruct((PEERS, 3, 2, BLOCK, 128), q.dtype)
    out_spec = pl.BlockSpec((2, 3, 2, BLOCK, 128), lambda i: (i, 0, 0, 0, 0))
    return pl.pallas_call(
        pack_kernel,
        grid=(8,),
        in_specs=[spec] * 4,
        out_specs=[out_spec] * 2,
        out_shape=[out] * 2,
        cost_estimate=pl.CostEstimate(flops=0, bytes_accessed=12 << 20, transcendentals=0),
        name="pack",
    )(q, k, v, g)


def unpack_kernel(slots_ref, og0_ref, og1_ref, kv0_ref, kv1_ref, o_ref, dq_ref, dk_ref, dv_ref):
    og_refs, kv_refs = (og0_ref, og1_ref), (kv0_ref, kv1_ref)
    for t in range(3):
        cols = slice(128 * t, 128 * t + 128)
        a, b = 2 * t, 2 * t + 1
        for part in range(2):
            rows = slice(BLOCK * part, BLOCK * part + BLOCK)
            og_a, og_b = og_refs[a // 3][a % 3, 0, part], og_refs[b // 3][b % 3, 0, part]
            kv_a, kv_b = kv_refs[a // 3][a % 3, 0, part], kv_refs[b // 3][b % 3, 0, part]
            dq_ref[rows, cols] = jnp.concatenate([og_a[:, :64], og_b[:, :64]], axis=1)
            o_ref[rows, cols] = jnp.concatenate([og_a[:, 64:], og_b[:, 64:]], axis=1)
            dk_ref[rows, cols] = jnp.concatenate([kv_a[:, :64], kv_b[:, :64]], axis=1)
            dv_ref[rows, cols] = jnp.concatenate([kv_a[:, 64:], kv_b[:, 64:]], axis=1)


def unpack(slots, og, kv):
    def spec(which):
        return pl.BlockSpec((3, 1, 2, BLOCK, 128), lambda i, slots: (0, slots[2 * i + which], 0, 0, 0))

    rows = 2 * BLOCK
    out_spec = pl.BlockSpec((rows, 384), lambda i, slots: (0, i))
    out = jax.ShapeDtypeStruct((rows, 3072), og.dtype)
    return pl.pallas_call(
        unpack_kernel,
        grid_spec=pltpu.PrefetchScalarGridSpec(
            num_scalar_prefetch=1,
            grid=(8,),
            in_specs=[spec(0), spec(1), spec(0), spec(1)],
            out_specs=[out_spec] * 4,
        ),
        out_shape=[out] * 4,
        cost_estimate=pl.CostEstimate(flops=0, bytes_accessed=12 << 20, transcendentals=0),
        name="unpack",
    )(slots, og, og, kv, kv)


def nt(a, b):
    return lax.dot_general(a, b, (((1,), (1,)), ((), ())), preferred_element_type=jnp.float32)


def fused_kernel(
    tab_ref, kv_src, qg_src, og_out, dkv_out,
    kvin, qgin, kvx, stage, kvw, kvt, terms, seg, ogs, dks, sums, back, near, sd0, sd1, ex0, ex1,
    in_send, in_recv, in_self, x_send, x_recv, b_send, b_recv, o_send, o_recv, o_self,
    *, heads, blocks, per_list,
):
    bf16, f32 = jnp.bfloat16, jnp.float32
    me, slab = lax.axis_index("seq"), lax.axis_index("slab")
    slabs = lax.axis_size("slab")
    z, x = me // 4, me % 4
    entries = blocks * per_list
    window = blocks + 2 * CROSS
    at_perm = heads * entries
    at_keep = 2 * at_perm
    at_last = 3 * at_perm
    at_asked = at_last + heads * window
    at_later = at_asked + 2 * CROSS
    at_earlier = at_later + blocks
    after = {"slab": (slab + 1) % slabs}
    before = {"slab": (slab + slabs - 1) % slabs}

    def peer(dz, dx):
        return (z + dz) % 4 * 4 + (x + dx) % 4

    def remote(src, dst, send, recv, device):
        return pltpu.make_async_remote_copy(
            src_ref=src, dst_ref=dst, send_sem=send, recv_sem=recv, device_id=device, device_id_type=MESH
        )

    barrier = pltpu.get_barrier_semaphore()
    for dz, dx in SPREAD:
        pl.semaphore_signal(barrier, 1, device_id={"seq": peer(dz, dx)}, device_id_type=MESH)
    for device in (after, before):
        pl.semaphore_signal(barrier, 1, device_id=device, device_id_type=MESH)
    pl.semaphore_wait(barrier, len(SPREAD) + 2)

    inputs = ((kv_src, kvin), (qg_src, qgin))
    for h in range(heads):
        for t, (src, dst) in enumerate(inputs):
            pltpu.make_async_copy(src.at[me, h], dst.at[h, pl.ds(0, 2)], in_self.at[t, h]).start()
            for dz, dx in SPREAD:
                there = dst.at[h, pl.ds(2 * slot_of(-dz, -dx), 2)]
                to = peer(dz, dx)
                remote(src.at[to, h], there, in_send.at[t, h], in_recv.at[t, h], {"seq": to}).start()

    def arrived(t, h):
        src, dst = inputs[t]
        pltpu.make_async_copy(src.at[me, h], dst.at[h, pl.ds(0, 2)], in_self.at[t, h]).wait()
        rest = dst.at[h, pl.ds(2, blocks - 2)]
        pltpu.make_async_copy(rest, rest, in_recv.at[t, h]).wait()

    def crossing(h, side):
        return remote(
            stage.at[h, pl.ds(CROSS * side, CROSS)], kvx.at[h, pl.ds(CROSS * side, CROSS)],
            x_send.at[h, side], x_recv.at[h, side], (after, before)[side],
        )

    def returning(h, side):
        return remote(
            sums.at[h, pl.ds(CROSS * side, CROSS)], back.at[h, pl.ds(CROSS * side, CROSS)],
            b_send.at[h, side], b_recv.at[h, side], (before, after)[side],
        )

    def open_window(h):
        arrived(0, h)

        @pl.loop(0, blocks)
        def _(w):
            kvw[w] = kvin[h, w]

        for c in range(2 * CROSS):
            stage[h, c] = kvw[tab_ref[at_asked + c]]

        @pl.loop(0, blocks)
        def _(w):
            kvt[w] = kvin[h, w].T

        for side in range(2):
            crossing(h, side).start()

    seg[entries] = jnp.zeros((BLOCK, 128), bf16)
    near[2 * CROSS] = jnp.zeros((BLOCK, 128), bf16)
    left = lax.broadcasted_iota(jnp.int32, (BLOCK, 128), 1) < HDIM
    open_window(0)

    def output(src, dst, t, h, p):
        rel = p * STEP % PEERS
        dz, dx = rel // 4, rel % 4
        there = slot_of(4 - dz, 4 - dx)
        return remote(src.at[h, pl.ds(2 * p, 2)], dst.at[h, there], o_send.at[t, h], o_recv.at[t, h], {"seq": peer(dz, dx)})

    def output_self(src, dst, t, h):
        return pltpu.make_async_copy(src.at[h, pl.ds(0, 2)], dst.at[h, 0], o_self.at[t, h])

    @pl.loop(0, heads)
    def _(h):
        for side in range(2):
            crossing(h, side).wait_recv()
        for c in range(2 * CROSS):
            block = kvx[h, c]
            kvw[blocks + c] = block
            kvt[blocks + c] = block.T
        arrived(1, h)

        @pl.loop(0, blocks // 2)
        def _(p):
            @pl.when(p == 1)
            def _():
                output_self(ogs, og_out, 0, h).start()

            @pl.when(p > 1)
            def _():
                output(ogs, og_out, 0, h, p - 1).start()

            pairs = []
            for half, (sd, ex) in enumerate(((sd0, ex0), (sd1, ex1))):
                b = 2 * p + half
                qg = qgin[h, b]
                zero = jnp.zeros_like(qg)
                both = jnp.concatenate([jnp.where(left, qg, zero), jnp.where(left, zero, qg)], axis=0)
                base = (h * blocks + b) * per_list
                ids = [tab_ref[base + j] for j in range(per_list)]
                top = None
                for j in range(per_list):
                    pair = nt(kvw[ids[j]], both)
                    sd[j] = pair
                    part = jnp.max(pair[:, :BLOCK].reshape(16, 8, BLOCK), axis=0)
                    top = part if top is None else jnp.maximum(top, part)
                pairs.append((b, sd, ex, both, ids, jnp.max(top, axis=0, keepdims=True)))
            for b, sd, ex, both, ids, row_max in pairs:
                total = jnp.zeros((8, BLOCK), f32)
                mixed = jnp.zeros((8, BLOCK), f32)
                for j in range(per_list):
                    e = jnp.exp(sd[j, :, :BLOCK] - row_max)
                    sd[j, :, :BLOCK] = e
                    ex[j, :, BLOCK:] = e.astype(bf16)
                    total += jnp.sum(e.reshape(16, 8, BLOCK), axis=0)
                    mixed += jnp.sum((e * sd[j, :, BLOCK:]).reshape(16, 8, BLOCK), axis=0)
                inverse = 1.0 / jnp.sum(total, axis=0, keepdims=True)
                correction = jnp.sum(mixed, axis=0, keepdims=True) * inverse
                for j in range(per_list):
                    ex[j, :, :BLOCK] = (sd[j, :, :BLOCK] * (sd[j, :, BLOCK:] - correction)).astype(bf16)
                out = jnp.zeros((128, 2 * BLOCK), f32)
                for j in range(0, per_list, 2):
                    lhs = jnp.concatenate([kvt[ids[j]], kvt[ids[j + 1]]], axis=1)
                    rhs = ex[j : j + 2].reshape(2 * BLOCK, 2 * BLOCK)
                    out += jnp.dot(lhs, rhs, preferred_element_type=f32)
                outs = jnp.concatenate([out[:HDIM, :BLOCK] * (inverse * SCALE), out[HDIM:, BLOCK:] * inverse], axis=0)
                ogs[h, b] = outs.T.astype(bf16)
                column = jnp.broadcast_to(inverse, (BLOCK, BLOCK)).T
                scaled = (both.astype(f32) * jnp.concatenate([column, column], axis=0)).astype(bf16)
                for j in range(per_list):
                    terms[b * per_list + j] = jnp.dot(ex[j], scaled, preferred_element_type=f32)

        @pl.when(h + 1 < heads)
        def _():
            open_window(h + 1)

        output(ogs, og_out, 0, h, blocks // 2 - 1).start()

        def running(t, acc):
            keep = tab_ref[at_keep + h * entries + t].astype(f32)
            acc = acc * keep + terms[tab_ref[at_perm + h * entries + t]]
            seg[t] = acc.astype(bf16)
            return acc

        lax.fori_loop(0, entries, running, jnp.zeros((BLOCK, 128), f32))
        last = at_last + h * window
        for c in range(2 * CROSS):
            sums[h, c] = seg[tab_ref[last + blocks + c]]
        for side in range(2):
            returning(h, side).start()
        for side in range(2):
            returning(h, side).wait_recv()
        for c in range(2 * CROSS):
            near[c] = back[h, c]

        @pl.loop(0, blocks)
        def _(w):
            total = seg[tab_ref[last + w]].astype(f32)
            total += near[tab_ref[at_later + w]].astype(f32)
            total += near[tab_ref[at_earlier + w]].astype(f32)
            dks[h, w] = total.astype(bf16)

        output_self(dks, dkv_out, 1, h).start()

        @pl.loop(1, blocks // 2)
        def _(p):
            output(dks, dkv_out, 1, h, p).start()

    for h in range(heads):
        for t, (src, dst) in enumerate(inputs):
            rest = dst.at[h, pl.ds(2, blocks - 2)]
            pltpu.make_async_copy(rest, rest, in_send.at[t, h]).wait()
        for side in range(2):
            crossing(h, side).wait_send()
            returning(h, side).wait_send()
        for t, (src, dst) in enumerate(((ogs, og_out), (dks, dkv_out))):
            output_self(src, dst, t, h).wait()
            rest = src.at[h, pl.ds(2, blocks - 2)]
            pltpu.make_async_copy(rest, rest, o_send.at[t, h]).wait()
            landed = dst.at[h, pl.ds(1, PEERS - 1)]
            pltpu.make_async_copy(landed, landed, o_recv.at[t, h]).wait()


def fused(tab, kv, qg, heads, blocks, per_list):
    f32, bf16 = jnp.float32, jnp.bfloat16
    window = blocks + 2 * CROSS
    entries = blocks * per_list
    block = (BLOCK, 128)
    sems = pltpu.SemaphoreType.DMA
    out = jax.ShapeDtypeStruct((heads, PEERS, 2, BLOCK, 128), bf16)
    any_spec = pl.BlockSpec(memory_space=pl.ANY)
    return pl.pallas_call(
        functools.partial(fused_kernel, heads=heads, blocks=blocks, per_list=per_list),
        in_specs=[pl.BlockSpec(memory_space=pltpu.SMEM), any_spec, any_spec],
        out_specs=[any_spec, any_spec],
        out_shape=[out, out],
        scratch_shapes=[
            pltpu.VMEM((heads, blocks, *block), bf16),
            pltpu.VMEM((heads, blocks, *block), bf16),
            pltpu.VMEM((heads, 2 * CROSS, *block), bf16),
            pltpu.VMEM((heads, 2 * CROSS, *block), bf16),
            pltpu.VMEM((window, *block), bf16),
            pltpu.VMEM((window, *block), bf16),
            pltpu.VMEM((entries, *block), f32),
            pltpu.VMEM((entries + 1, *block), bf16),
            pltpu.VMEM((heads, blocks, *block), bf16),
            pltpu.VMEM((heads, blocks, *block), bf16),
            pltpu.VMEM((heads, 2 * CROSS, *block), bf16),
            pltpu.VMEM((heads, 2 * CROSS, *block), bf16),
            pltpu.VMEM((2 * CROSS + 1, *block), bf16),
            pltpu.VMEM((per_list, BLOCK, 2 * BLOCK), f32),
            pltpu.VMEM((per_list, BLOCK, 2 * BLOCK), f32),
            pltpu.VMEM((per_list, BLOCK, 2 * BLOCK), bf16),
            pltpu.VMEM((per_list, BLOCK, 2 * BLOCK), bf16),
        ]
        + [sems((2, heads))] * 3
        + [sems((heads, 2))] * 4
        + [sems((2, heads))] * 3,
        compiler_params=pltpu.CompilerParams(
            collective_id=0, has_side_effects=True, vmem_limit_bytes=60 << 20
        ),
        name="fused",
    )(tab, kv, qg)


def first_hits(pattern, base, blocks):
    ids = jnp.arange(blocks, dtype=jnp.int32)
    hits = jnp.any(pattern.reshape(-1)[:, None] == (base + ids)[None, :], axis=0)
    rank = jnp.sum(jnp.where(ids[None, :] <= ids[:, None], hits[None, :].astype(jnp.int32), 0), axis=1)
    slots = jnp.arange(CROSS, dtype=jnp.int32)
    chosen = hits[None, :] & (rank[None, :] == slots[:, None] + 1)
    return jnp.sum(jnp.where(chosen, ids[None, :], 0), axis=1)


def local(query, key, value, d_out, pattern):
    heads, blocks, per_list = pattern.shape
    i32 = jnp.int32
    own_base = lax.axis_index("slab") * blocks
    me = lax.axis_index("seq")
    z, x = me // 4, me % 4
    need_prev = first_hits(pattern, own_base - blocks, blocks)
    need_next = first_hits(pattern, own_base + blocks, blocks)
    asked_next = from_behind(need_prev, "slab", -1)
    asked_prev = from_behind(need_next, "slab", 1)
    kv, qg = pack(query, key, value, d_out)

    def place(block):
        source = block // 2
        return 2 * slot_of(source // 4 - z + 4, source % 4 - x + 4) + block % 2

    slots = jnp.arange(CROSS, dtype=i32)
    pos_prev = jnp.min(jnp.where(pattern[..., None] == own_base - blocks + need_prev, slots, CROSS - 1), axis=-1)
    pos_next = jnp.min(jnp.where(pattern[..., None] == own_base + blocks + need_next, slots, CROSS - 1), axis=-1)
    relative = pattern - own_base
    ids = jnp.where(
        relative < 0, blocks + pos_prev, jnp.where(relative < blocks, place(relative), blocks + CROSS + pos_next)
    )
    every = jnp.arange(blocks, dtype=i32)
    where_to = place(every)
    ids = jnp.sum(jnp.where((where_to[None, :] == every[:, None])[None, :, :, None], ids[:, None], 0), axis=2)
    flat = ids.reshape(heads, -1)
    entries = blocks * per_list
    number = jnp.arange(entries, dtype=i32)
    order = flat * entries + number
    rank = jnp.sum((order[:, None, :] < order[:, :, None]).astype(i32), axis=2)
    lands = rank[:, None, :] == number[None, :, None]
    perm = jnp.sum(jnp.where(lands, number, 0), axis=2)
    ranked = jnp.sum(jnp.where(lands, flat[:, None, :], 0), axis=2)
    keep = jnp.concatenate([jnp.zeros((heads, 1), i32), (ranked[:, 1:] == ranked[:, :-1]).astype(i32)], axis=1)
    spots = jnp.arange(blocks + 2 * CROSS, dtype=i32)
    upto = jnp.sum((flat[:, None, :] <= spots[None, :, None]).astype(i32), axis=2)
    held = jnp.any(flat[:, None, :] == spots[None, :, None], axis=2)
    last = jnp.where(held, upto - 1, entries)
    later, earlier = place(asked_next), place(asked_prev)

    def returned(asked, first):
        return jnp.min(jnp.where(asked[None, :] == every[:, None], first + slots, 2 * CROSS), axis=1)

    tab = jnp.concatenate(
        [a.reshape(-1) for a in (ids, perm, keep, last, later, earlier, returned(later, 0), returned(earlier, CROSS))]
    )
    og, dkv = fused(tab, kv, qg, heads, blocks, per_list)
    group = jnp.arange(PEERS, dtype=i32)
    return tuple(unpack(slot_of(group // 4 - z + 4, group % 4 - x + 4), og, dkv))


def solution(mesh):
    rows = P(("slab", "seq"), None)
    return jax.shard_map(
        local,
        mesh=mesh,
        in_specs=(rows, rows, rows, rows, P("seq", "slab", None)),
        out_specs=(rows, rows, rows, rows),
        check_vma=False,
    )
```

time: 307 us -> 189 us (0.62)
  the two profiles are of different devices: /device:TPU:0 before, /device:TPU:55 now
where the time goes in v1:
time: 189 us; the launch traced here: 188 us
  Pallas kernels  174 us (92%)
  other arithmetic  5.87 us (3%)
  starting transfers between devices  5.56 us (3%)
    pallas_call x1, Pallas kernels, fused(): pl.pallas_call(functools.partial(fused_kernel, heads=heads, blocks=blocks...  156 us
    pallas_call x1, Pallas kernels, unpack(): pl.pallas_call(unpack_kernel, grid_spec=pltpu.PrefetchScalarGridSpec(num_...  9.47 us
    pallas_call x1, Pallas kernels, pack(): pl.pallas_call(pack_kernel, grid=(8,), in_specs=[spec] * 4, out_specs=[ou...  8.81 us
    ppermute x2, starting transfers between devices, from_behind(): return lax.ppermute(x, axis, pairs)  5.56 us
  transfers between devices with their start and end apart: 2, of which 0 were waited for; matrix products, arithmetic and copies ran while one was open for 3% of the time, Pallas kernels for 5%

profile of v1, /device:TPU:55, one launch (start us, length us, event | category | flops | bytes accessed | tf_op | source)
XLA Modules:
  0.0 188.0 jit_solution(4356422027617944236)
XLA Ops:
  0.6 0.8 copy.14
  1.4 0.1 eq.188
  1.5 0.2 compare_reduce_fusion.1
  1.8 0.1 select_reduce_fusion.6
  1.9 0.1 select_reduce_fusion.5
  2.0 0.2 select_reduce_fusion.10
  2.2 2.6 %collective-permute-start = (s32[4]{0:T(128)S(1)}, s32[4]{0:T(128)S(1)}, u32[]{:S(2)}, u32[]{:S(2)}) collective-permute-start(s32[4]{0:T(128)S(1)} %get-tuple-element.18), channel_id=1, source_target_pairs={{16,0},{32,16},{48,32},{64,48},{80,64},{96,80},{112,96},{17,1},{33... | collective-permute-start | bytes 56 | tf_op jit(solution)/shard_map/ppermute | solution.py:23
  4.8 3.0 %collective-permute-start.1 = (s32[4]{0:T(128)S(1)}, s32[4]{0:T(128)S(1)}, u32[]{:S(2)}, u32[]{:S(2)}) collective-permute-start(s32[4]{0:T(128)S(1)} %get-tuple-element.19), channel_id=1, source_target_pairs={{0,16},{16,32},{32,48},{48,64},{64,80},{80,96},{96,112},{1,17},{17... | collective-permute-start | bytes 56 | tf_op jit(solution)/shard_map/ppermute | solution.py:23
  7.8 0.6 and_select_fusion.21.slots_ref
  8.4 0.8 select_reduce_fusion.4
  9.2 0.8 fusion.14
  10.0 1.7 select_reduce_fusion.2
  11.7 0.1 reshape.201
  11.7 0.1 reshape.200
  11.8 0.1 fusion
  12.0 0.2 convert_reduce_fusion.1
  12.2 0.1 select_n.267
  12.2 0.3 convert_reduce_fusion
  12.6 0.4 select_reduce_fusion
  12.9 0.1 slice_compare_fusion
  13.0 0.1 pad_convert_fusion
  13.1 8.8 %pack.1 = (bf16[16,3,2,128,128]{4,3,2,1,0:T(8,128)(2,1)}, bf16[16,3,2,128,128]{4,3,2,1,0:T(8,128)(2,1)}) custom-call(bf16[256,3072]{1,0:T(8,128)(2,1)} %q_ref.1, bf16[256,3072]{1,0:T(8,128)(2,1)} %k_ref.1, bf16[256,3072]{1,0:T(8,128)(2,1)} %v_ref.1, bf16[256,3072]{1,0:T(8,128)(2,1)} %g_ref.1), custom_call_target="tpu_custom_call" | custom-call | bytes 12582912 | tf_op jit(solution)/shard_map/pack/pallas_call | solution.py:51
  21.9 0.0 collective-permute-done
  21.9 0.1 select_reduce_fusion.8
  22.0 0.0 collective-permute-done.1
  22.1 0.1 select_reduce_fusion.7
  22.2 0.7 concatenate.7.tab_ref
  22.8 155.7 %fused.1 = (bf16[3,16,2,128,128]{4,3,2,1,0:T(8,128)(2,1)}, bf16[3,16,2,128,128]{4,3,2,1,0:T(8,128)(2,1)}) custom-call(s32[2496]{0:T(1024)} %concatenate.7.tab_ref, bf16[16,3,2,128,128]{4,3,2,1,0:T(8,128)(2,1)} %get-tuple-element.8.kv_src, bf16[16,3,2,128,128]{4,3,2,1,0:T(8,128)(2,1)} %get-tuple-element.9.qg_src), custom_call_target="tpu_custom_call" | custom-call | tf_op jit(solution)/shard_map/fused/pallas_call | solution.py:315
  178.5 9.5 %unpack.1 = (bf16[256,3072]{1,0:T(8,128)(2,1)}, bf16[256,3072]{1,0:T(8,128)(2,1)}, bf16[256,3072]{1,0:T(8,128)(2,1)}, bf16[256,3072]{1,0:T(8,128)(2,1)}) custom-call(s32[16]{0:T(128)} %and_select_fusion.21.slots_ref, bf16[3,16,2,128,128]{4,3,2,1,0:T(8,128)(2,1)} %get-tuple-element.10.og0_ref.og1_ref, ...), custom_call_target="tpu_custom_call" | custom-call | bytes 12582912 | tf_op jit(solution)/shard_map/unpack/pallas_call | solution.py:84
  (15 shorter events, 0.2 us)
Async XLA Ops:
  2.2 19.7 %collective-permute-start = (s32[4]{0:T(128)S(1)}, s32[4]{0:T(128)S(1)}, u32[]{:S(2)}, u32[]{:S(2)}) collective-permute-start(s32[4]{0:T(128)S(1)} %get-tuple-element.18), channel_id=1, source_target_pairs={{16,0},{32,16},{48,32},{64,48},{80,64},{96,80},{112,96},{17,1},{33... | collective-permute-start | bytes 56 | tf_op jit(solution)/shard_map/ppermute | solution.py:23
  4.8 17.3 %collective-permute-start.1 = (s32[4]{0:T(128)S(1)}, s32[4]{0:T(128)S(1)}, u32[]{:S(2)}, u32[]{:S(2)}) collective-permute-start(s32[4]{0:T(128)S(1)} %get-tuple-element.19), channel_id=1, source_target_pairs={{0,16},{16,32},{32,48},{48,64},{64,80},{80,96},{96,112},{1,17},{17... | collective-permute-start | bytes 56 | tf_op jit(solution)/shard_map/ppermute | solution.py:23

commit v2 on v1

v2 whole, which is shorter than its diff:
```python
import functools

import jax
import jax.numpy as jnp
from jax import lax
from jax.experimental import pallas as pl
from jax.experimental.pallas import tpu as pltpu
from jax.sharding import PartitionSpec as P

CROSS = 4
HDIM = 64
BLOCK = 128
SCALE = HDIM**-0.5
PEERS = 16
STEP = 7
MESH = pl.DeviceIdType.MESH
SPREAD = ((0, 1), (1, 0), (0, 3), (3, 0), (1, 1), (3, 3), (1, 3), (3, 1), (0, 2), (2, 0), (1, 2), (2, 1), (3, 2), (2, 3), (2, 2))


def slot_of(dz, dx):
    return ((dz % 4) * 4 + dx % 4) * STEP % PEERS


def unpack_kernel(slots_ref, og0_ref, og1_ref, kv0_ref, kv1_ref, o_ref, dq_ref, dk_ref, dv_ref):
    og_refs, kv_refs = (og0_ref, og1_ref), (kv0_ref, kv1_ref)
    for t in range(3):
        cols = slice(128 * t, 128 * t + 128)
        a, b = 2 * t, 2 * t + 1
        for part in range(2):
            rows = slice(BLOCK * part, BLOCK * part + BLOCK)
            og_a, og_b = og_refs[a // 3][a % 3, 0, part], og_refs[b // 3][b % 3, 0, part]
            kv_a, kv_b = kv_refs[a // 3][a % 3, 0, part], kv_refs[b // 3][b % 3, 0, part]
            dq_ref[rows, cols] = jnp.concatenate([og_a[:, :64], og_b[:, :64]], axis=1)
            o_ref[rows, cols] = jnp.concatenate([og_a[:, 64:], og_b[:, 64:]], axis=1)
            dk_ref[rows, cols] = jnp.concatenate([kv_a[:, :64], kv_b[:, :64]], axis=1)
            dv_ref[rows, cols] = jnp.concatenate([kv_a[:, 64:], kv_b[:, 64:]], axis=1)


def unpack(slots, og, kv):
    def spec(which):
        return pl.BlockSpec((3, 1, 2, BLOCK, 128), lambda i, slots: (0, slots[2 * i + which], 0, 0, 0))

    rows = 2 * BLOCK
    out_spec = pl.BlockSpec((rows, 384), lambda i, slots: (0, i))
    out = jax.ShapeDtypeStruct((rows, 3072), og.dtype)
    return pl.pallas_call(
        unpack_kernel,
        grid_spec=pltpu.PrefetchScalarGridSpec(
            num_scalar_prefetch=1,
            grid=(8,),
            in_specs=[spec(0), spec(1), spec(0), spec(1)],
            out_specs=[out_spec] * 4,
        ),
        out_shape=[out] * 4,
        cost_estimate=pl.CostEstimate(flops=0, bytes_accessed=12 << 20, transcendentals=0),
        name="unpack",
    )(slots, og, og, kv, kv)


def nt(a, b):
    return lax.dot_general(a, b, (((1,), (1,)), ((), ())), preferred_element_type=jnp.float32)


def turned(row, size):
    return jnp.broadcast_to(row, (size, size)).T


def plan(pat_ref, tab_ref, ask_ref, base, z, x, heads, blocks, per_list):
    i32 = jnp.int32
    entries = blocks * per_list

    def grid(rows, columns, dim):
        return lax.broadcasted_iota(i32, (rows, columns), dim)

    def total(picked, value):
        return jnp.sum(jnp.where(picked, value, 0), axis=0, keepdims=True)

    def place(block):
        source = block >> 1
        rel = ((((source >> 2) - z) & 3) << 2) + (((source & 3) - x) & 3)
        return (((rel * STEP) & (PEERS - 1)) << 1) + (block & 1)

    rows = []
    hits = [jnp.zeros((1, 128), i32), jnp.zeros((1, 128), i32)]
    spot = grid(entries, 128, 1)
    for h in range(heads):
        pattern = pat_ref[h]
        lane = grid(blocks, entries, 1)
        spread = jnp.zeros((blocks, entries), i32)
        for j in range(per_list):
            spread = jnp.where((lane & (per_list - 1)) == j, pattern[:, j : j + 1], spread)
        mine = (lane >> 3) == grid(blocks, entries, 0)
        rows.append(total(mine, spread) - base)
        column = turned(rows[h], entries)[:, :128]
        for side, shift in enumerate((-blocks, blocks)):
            found = (column == spot + shift) & (spot < blocks)
            hits[side] = jnp.maximum(hits[side], jnp.max(found.astype(i32), axis=0, keepdims=True))
    down, across = grid(128, 128, 0), grid(128, 128, 1)
    ranks = []
    for side in range(2):
        hit = turned(hits[side], 128)
        rank = turned(total(down <= across, hit), 128)
        ranks.append(rank)
        ask_ref[side, 0:1] = total((hit > 0) & (rank == across + 1), place(down))
        back = jnp.where(hit > 0, rank - 1 + CROSS * side, 2 * CROSS)
        ask_ref[side, 1:2] = total((place(down) == across) & (down < blocks), back)
    number = grid(1, entries, 1)
    order = grid(entries, entries, 1)
    for h in range(heads):
        row = rows[h]
        block = grid(128, entries, 0)
        column = [jnp.concatenate([rank, rank], axis=1) for rank in ranks]
        outside = [total(block == row + shift, column[side] - 1) for side, shift in enumerate((blocks, -blocks))]
        ids = jnp.where(
            row < 0, blocks + outside[0], jnp.where(row < blocks, place(row), blocks + CROSS + outside[1])
        )
        key = ids * entries + number
        rank = total(turned(key, entries) < key, 1)
        column, rank = turned(ids, entries), turned(rank, entries)
        lands = rank == order
        ranked = total(lands, column)
        ahead = total(rank + 1 == order, column)
        tab_ref[h, 0:1] = ids
        tab_ref[h, 1:2] = total(lands, grid(entries, entries, 0))
        tab_ref[h, 2:3] = jnp.where((ranked == ahead) & (number > 0), 1, 0)
        upto = total(column <= order, 1)
        held = total(column == order, 1)
        tab_ref[h, 3:4] = jnp.where(held > 0, upto - 1, entries)


def fused_kernel(
    pat_ref, q_src, k_src, v_src, g_src, og_out, dkv_out,
    raw_q, raw_k, raw_v, raw_g, tabv, tab, askv, gotv, got,
    kvin, qgin, kvx, stage, kvw, kvt, terms, seg, ogs, dks, sums, back, near, sd0, sd1, ex0, ex1,
    in_send, in_recv, in_self, x_send, x_recv, b_send, b_recv, o_send, o_recv, o_self,
    raw_sem, tab_sem, got_sem, a_send, a_recv,
    *, heads, blocks, per_list,
):
    bf16, f32 = jnp.bfloat16, jnp.float32
    me, slab = lax.axis_index("seq"), lax.axis_index("slab")
    slabs = lax.axis_size("slab")
    z, x = me // 4, me % 4
    entries = blocks * per_list
    after = {"slab": (slab + 1) % slabs}
    before = {"slab": (slab + slabs - 1) % slabs}

    def peer(dz, dx):
        return (z + dz) % 4 * 4 + (x + dx) % 4

    def remote(src, dst, send, recv, device):
        return pltpu.make_async_remote_copy(
            src_ref=src, dst_ref=dst, send_sem=send, recv_sem=recv, device_id=device, device_id_type=MESH
        )

    raws = ((k_src, raw_k), (v_src, raw_v), (q_src, raw_q), (g_src, raw_g))
    loads = [pltpu.make_async_copy(src, dst, raw_sem.at[i]) for i, (src, dst) in enumerate(raws)]
    for load in loads:
        load.start()
    barrier = pltpu.get_barrier_semaphore()
    for dz, dx in SPREAD:
        pl.semaphore_signal(barrier, 1, device_id={"seq": peer(dz, dx)}, device_id_type=MESH)
    for device in (after, before):
        pl.semaphore_signal(barrier, 1, device_id=device, device_id_type=MESH)
    pl.semaphore_wait(barrier, len(SPREAD) + 2)

    inputs = ((raw_k, raw_v, dks, kvin), (raw_q, raw_g, ogs, qgin))

    def input_self(t, h):
        return pltpu.make_async_copy(
            inputs[t][2].at[h, pl.ds(0, 2)], inputs[t][3].at[h, pl.ds(0, 2)], in_self.at[t, h]
        )

    def send_input(t, h, p):
        rel = p * STEP % PEERS
        dz, dx = rel // 4, rel % 4
        there = inputs[t][3].at[h, pl.ds(2 * slot_of(4 - dz, 4 - dx), 2)]
        src = inputs[t][2].at[h, pl.ds(2 * p, 2)]
        remote(src, there, in_send.at[t, h], in_recv.at[t, h], {"seq": peer(dz, dx)}).start()

    for h in range(heads):
        for t in range(2):
            if h == 0:
                loads[2 * t].wait()
                loads[2 * t + 1].wait()
            one, two, packed, _ = inputs[t]

            @pl.loop(0, PEERS)
            def _(p):
                rel = p * STEP % PEERS
                column = 3 * peer(rel // 4, rel % 4) + h
                lanes = pl.ds(pl.multiple_of(column // 2 * 128, 128), 128)

                for side in range(2):

                    @pl.when(column % 2 == side)
                    def _():
                        half = slice(HDIM * side, HDIM * side + HDIM)
                        for part in range(2):
                            rows = pl.ds(BLOCK * part, BLOCK)
                            a, b = one[rows, lanes], two[rows, lanes]
                            if t == 1:
                                a = a * jnp.asarray(SCALE, bf16)
                            packed[h, 2 * p + part] = jnp.concatenate([a[:, half], b[:, half]], axis=1)

                @pl.when(p == 1)
                def _():
                    input_self(t, h).start()

                @pl.when(p > 1)
                def _():
                    send_input(t, h, p - 1)

            send_input(t, h, PEERS - 1)

    def arrived(t, h):
        input_self(t, h).wait()
        rest = inputs[t][3].at[h, pl.ds(2, blocks - 2)]
        pltpu.make_async_copy(rest, rest, in_recv.at[t, h]).wait()

    def sent(t, h):
        rest = inputs[t][2].at[h, pl.ds(2, blocks - 2)]
        pltpu.make_async_copy(rest, rest, in_send.at[t, h]).wait()

    plan(pat_ref, tabv, askv, slab * blocks, z, x, heads, blocks, per_list)
    asking = [remote(askv.at[i], gotv.at[i], a_send.at[i], a_recv.at[i], (before, after)[i]) for i in range(2)]
    for ask in asking:
        ask.start()
    table = pltpu.make_async_copy(tabv, tab, tab_sem.at[0])
    table.start()
    for ask in asking:
        ask.wait()
    gotten = pltpu.make_async_copy(gotv, got, got_sem.at[0])
    gotten.start()
    table.wait()
    gotten.wait()

    def crossing(h, side):
        return remote(
            stage.at[h, pl.ds(CROSS * side, CROSS)], kvx.at[h, pl.ds(CROSS * side, CROSS)],
            x_send.at[h, side], x_recv.at[h, side], (after, before)[side],
        )

    def returning(h, side):
        return remote(
            sums.at[h, pl.ds(CROSS * side, CROSS)], back.at[h, pl.ds(CROSS * side, CROSS)],
            b_send.at[h, side], b_recv.at[h, side], (before, after)[side],
        )

    def open_window(h):
        arrived(0, h)

        @pl.loop(0, blocks)
        def _(w):
            kvw[w] = kvin[h, w]

        for c in range(2 * CROSS):
            stage[h, c] = kvw[got[c // CROSS, 0, c % CROSS]]

        @pl.loop(0, blocks)
        def _(w):
            kvt[w] = kvin[h, w].T

        for side in range(2):
            crossing(h, side).start()

    seg[entries] = jnp.zeros((BLOCK, 128), bf16)
    near[2 * CROSS] = jnp.zeros((BLOCK, 128), bf16)
    left = lax.broadcasted_iota(jnp.int32, (BLOCK, 128), 1) < HDIM
    open_window(0)

    def output(src, dst, t, h, p):
        rel = p * STEP % PEERS
        dz, dx = rel // 4, rel % 4
        there = slot_of(4 - dz, 4 - dx)
        return remote(src.at[h, pl.ds(2 * p, 2)], dst.at[h, there], o_send.at[t, h], o_recv.at[t, h], {"seq": peer(dz, dx)})

    def output_self(src, dst, t, h):
        return pltpu.make_async_copy(src.at[h, pl.ds(0, 2)], dst.at[h, 0], o_self.at[t, h])

    @pl.loop(0, heads)
    def _(h):
        for side in range(2):
            crossing(h, side).wait_recv()
        for c in range(2 * CROSS):
            block = kvx[h, c]
            kvw[blocks + c] = block
            kvt[blocks + c] = block.T
        arrived(1, h)
        sent(0, h)
        sent(1, h)

        @pl.loop(0, blocks // 2)
        def _(p):
            @pl.when(p == 1)
            def _():
                output_self(ogs, og_out, 0, h).start()

            @pl.when(p > 1)
            def _():
                output(ogs, og_out, 0, h, p - 1).start()

            rel = p * STEP % PEERS
            first = 2 * per_list * peer(rel // 4, rel % 4)
            pairs = []
            for half, (sd, ex) in enumerate(((sd0, ex0), (sd1, ex1))):
                b = 2 * p + half
                qg = qgin[h, b]
                zero = jnp.zeros_like(qg)
                both = jnp.concatenate([jnp.where(left, qg, zero), jnp.where(left, zero, qg)], axis=0)
                base = first + half * per_list
                ids = [tab[h, 0, base + j] for j in range(per_list)]
                top = None
                for j in range(per_list):
                    pair = nt(kvw[ids[j]], both)
                    sd[j] = pair
                    part = jnp.max(pair[:, :BLOCK].reshape(16, 8, BLOCK), axis=0)
                    top = part if top is None else jnp.maximum(top, part)
                pairs.append((b, base, sd, ex, both, ids, jnp.max(top, axis=0, keepdims=True)))
            for b, base, sd, ex, both, ids, row_max in pairs:
                total = jnp.zeros((8, BLOCK), f32)
                mixed = jnp.zeros((8, BLOCK), f32)
                for j in range(per_list):
                    e = jnp.exp(sd[j, :, :BLOCK] - row_max)
                    sd[j, :, :BLOCK] = e
                    ex[j, :, BLOCK:] = e.astype(bf16)
                    total += jnp.sum(e.reshape(16, 8, BLOCK), axis=0)
                    mixed += jnp.sum((e * sd[j, :, BLOCK:]).reshape(16, 8, BLOCK), axis=0)
                inverse = 1.0 / jnp.sum(total, axis=0, keepdims=True)
                correction = jnp.sum(mixed, axis=0, keepdims=True) * inverse
                for j in range(per_list):
                    ex[j, :, :BLOCK] = (sd[j, :, :BLOCK] * (sd[j, :, BLOCK:] - correction)).astype(bf16)
                out = jnp.zeros((128, 2 * BLOCK), f32)
                for j in range(0, per_list, 2):
                    lhs = jnp.concatenate([kvt[ids[j]], kvt[ids[j + 1]]], axis=1)
                    rhs = ex[j : j + 2].reshape(2 * BLOCK, 2 * BLOCK)
                    out += jnp.dot(lhs, rhs, preferred_element_type=f32)
                outs = jnp.concatenate([out[:HDIM, :BLOCK] * (inverse * SCALE), out[HDIM:, BLOCK:] * inverse], axis=0)
                ogs[h, b] = outs.T.astype(bf16)
                column = jnp.broadcast_to(inverse, (BLOCK, BLOCK)).T
                scaled = (both.astype(f32) * jnp.concatenate([column, column], axis=0)).astype(bf16)
                for j in range(per_list):
                    terms[base + j] = jnp.dot(ex[j], scaled, preferred_element_type=f32)

        @pl.when(h + 1 < heads)
        def _():
            open_window(h + 1)

        output(ogs, og_out, 0, h, blocks // 2 - 1).start()

        def running(t, acc):
            keep = tab[h, 2, t].astype(f32)
            acc = acc * keep + terms[tab[h, 1, t]]
            seg[t] = acc.astype(bf16)
            return acc

        lax.fori_loop(0, entries, running, jnp.zeros((BLOCK, 128), f32))
        for c in range(2 * CROSS):
            sums[h, c] = seg[tab[h, 3, blocks + c]]
        for side in range(2):
            returning(h, side).start()
        for side in range(2):
            returning(h, side).wait_recv()
        for c in range(2 * CROSS):
            near[c] = back[h, c]

        @pl.loop(0, blocks)
        def _(w):
            total = seg[tab[h, 3, w]].astype(f32)
            total += near[got[0, 1, w]].astype(f32)
            total += near[got[1, 1, w]].astype(f32)
            dks[h, w] = total.astype(bf16)

        output_self(dks, dkv_out, 1, h).start()

        @pl.loop(1, blocks // 2)
        def _(p):
            output(dks, dkv_out, 1, h, p).start()

    for h in range(heads):
        for side in range(2):
            crossing(h, side).wait_send()
            returning(h, side).wait_send()
        for t, (src, dst) in enumerate(((ogs, og_out), (dks, dkv_out))):
            output_self(src, dst, t, h).wait()
            rest = src.at[h, pl.ds(2, blocks - 2)]
            pltpu.make_async_copy(rest, rest, o_send.at[t, h]).wait()
            landed = dst.at[h, pl.ds(1, PEERS - 1)]
            pltpu.make_async_copy(landed, landed, o_recv.at[t, h]).wait()


def fused(pattern, q, k, v, g):
    heads, blocks, per_list = pattern.shape
    f32, bf16 = jnp.float32, jnp.bfloat16
    window = blocks + 2 * CROSS
    entries = blocks * per_list
    block = (BLOCK, 128)
    sems = pltpu.SemaphoreType.DMA
    out = jax.ShapeDtypeStruct((heads, PEERS, 2, BLOCK, 128), bf16)
    any_spec = pl.BlockSpec(memory_space=pl.ANY)
    return pl.pallas_call(
        functools.partial(fused_kernel, heads=heads, blocks=blocks, per_list=per_list),
        in_specs=[pl.BlockSpec(memory_space=pltpu.VMEM)] + [any_spec] * 4,
        out_specs=[any_spec, any_spec],
        out_shape=[out, out],
        scratch_shapes=[pltpu.VMEM(q.shape, bf16)] * 4
        + [
            pltpu.VMEM((heads, 8, entries), jnp.int32),
            pltpu.SMEM((heads, 8, entries), jnp.int32),
            pltpu.VMEM((2, 8, 128), jnp.int32),
            pltpu.VMEM((2, 8, 128), jnp.int32),
            pltpu.SMEM((2, 8, 128), jnp.int32),
            pltpu.VMEM((heads, blocks, *block), bf16),
            pltpu.VMEM((heads, blocks, *block), bf16),
            pltpu.VMEM((heads, 2 * CROSS, *block), bf16),
            pltpu.VMEM((heads, 2 * CROSS, *block), bf16),
            pltpu.VMEM((window, *block), bf16),
            pltpu.VMEM((window, *block), bf16),
            pltpu.VMEM((entries, *block), f32),
            pltpu.VMEM((entries + 1, *block), bf16),
            pltpu.VMEM((heads, blocks, *block), bf16),
            pltpu.VMEM((heads, blocks, *block), bf16),
            pltpu.VMEM((heads, 2 * CROSS, *block), bf16),
            pltpu.VMEM((heads, 2 * CROSS, *block), bf16),
            pltpu.VMEM((2 * CROSS + 1, *block), bf16),
            pltpu.VMEM((per_list, BLOCK, 2 * BLOCK), f32),
            pltpu.VMEM((per_list, BLOCK, 2 * BLOCK), f32),
            pltpu.VMEM((per_list, BLOCK, 2 * BLOCK), bf16),
            pltpu.VMEM((per_list, BLOCK, 2 * BLOCK), bf16),
        ]
        + [sems((2, heads))] * 3
        + [sems((heads, 2))] * 4
        + [sems((2, heads))] * 3
        + [sems((4,)), sems((1,)), sems((1,)), sems((2,)), sems((2,))],
        compiler_params=pltpu.CompilerParams(
            collective_id=0, has_side_effects=True, vmem_limit_bytes=60 << 20
        ),
        name="fused",
    )(pattern, q, k, v, g)


def local(query, key, value, d_out, pattern):
    me = lax.axis_index("seq")
    z, x = me // 4, me % 4
    og, dkv = fused(pattern, query, key, value, d_out)
    group = jnp.arange(PEERS, dtype=jnp.int32)
    return tuple(unpack(slot_of(group // 4 - z + 4, group % 4 - x + 4), og, dkv))


def solution(mesh):
    rows = P(("slab", "seq"), None)
    return jax.shard_map(
        local,
        mesh=mesh,
        in_specs=(rows, rows, rows, rows, P("seq", "slab", None)),
        out_specs=(rows, rows, rows, rows),
        check_vma=False,
    )
```

time: 189 us -> 167 us (0.88)
  the two profiles are of different devices: /device:TPU:55 before, /device:TPU:0 now
where the time goes in v2:
time: 167 us; the launch traced here: 166 us
  Pallas kernels  164 us (98%)
    pallas_call x1, Pallas kernels, fused(): pl.pallas_call(functools.partial(fused_kernel, heads=heads, blocks=blocks...  154 us
    pallas_call x1, Pallas kernels, unpack(): pl.pallas_call(unpack_kernel, grid_spec=pltpu.PrefetchScalarGridSpec(num_...  9.47 us

profile of v2, /device:TPU:0, one launch (start us, length us, event | category | flops | bytes accessed | tf_op | source)
XLA Modules:
  0.0 166.2 jit_solution(9855910924821837790)
XLA Ops:
  0.7 0.6 and_select_fusion.slots_ref
  1.2 1.4 copy.9.pat_ref
  2.6 154.1 %fused.1 = (bf16[3,16,2,128,128]{4,3,2,1,0:T(8,128)(2,1)}, bf16[3,16,2,128,128]{4,3,2,1,0:T(8,128)(2,1)}) custom-call(s32[3,32,8]{2,1,0:T(8,128)} %copy.9.pat_ref, bf16[256,3072]{1,0:T(8,128)(2,1)} %q_src.1, bf16[256,3072]{1,0:T(8,128)(2,1)} %k_src.1, bf16[256,3072]{1,0:T(8,128)(2,1)} %v_src.1, bf16[256,3072]{1,0:T(8,128)(2,1)} %g_src.1), custom_call_target="tpu_custom_call" | custom-call | tf_op jit(solution)/shard_map/fused/pallas_call | solution.py:400
  156.7 9.5 %unpack.1 = (bf16[256,3072]{1,0:T(8,128)(2,1)}, bf16[256,3072]{1,0:T(8,128)(2,1)}, bf16[256,3072]{1,0:T(8,128)(2,1)}, bf16[256,3072]{1,0:T(8,128)(2,1)}) custom-call(s32[16]{0:T(128)} %and_select_fusion.slots_ref, bf16[3,16,2,128,128]{4,3,2,1,0:T(8,128)(2,1)} %get-tuple-element.6.og0_ref.og1_ref, ...), custom_call_target="tpu_custom_call" | custom-call | bytes 12582912 | tf_op jit(solution)/shard_map/unpack/pallas_call | solution.py:46

commit v3 on v2

--- a/solution.py
+++ b/solution.py
@@ -21,40 +21,57 @@
     return ((dz % 4) * 4 + dx % 4) * STEP % PEERS
 
 
-def unpack_kernel(slots_ref, og0_ref, og1_ref, kv0_ref, kv1_ref, o_ref, dq_ref, dk_ref, dv_ref):
-    og_refs, kv_refs = (og0_ref, og1_ref), (kv0_ref, kv1_ref)
-    for t in range(3):
-        cols = slice(128 * t, 128 * t + 128)
-        a, b = 2 * t, 2 * t + 1
-        for part in range(2):
-            rows = slice(BLOCK * part, BLOCK * part + BLOCK)
-            og_a, og_b = og_refs[a // 3][a % 3, 0, part], og_refs[b // 3][b % 3, 0, part]
-            kv_a, kv_b = kv_refs[a // 3][a % 3, 0, part], kv_refs[b // 3][b % 3, 0, part]
-            dq_ref[rows, cols] = jnp.concatenate([og_a[:, :64], og_b[:, :64]], axis=1)
-            o_ref[rows, cols] = jnp.concatenate([og_a[:, 64:], og_b[:, 64:]], axis=1)
-            dk_ref[rows, cols] = jnp.concatenate([kv_a[:, :64], kv_b[:, :64]], axis=1)
-            dv_ref[rows, cols] = jnp.concatenate([kv_a[:, 64:], kv_b[:, 64:]], axis=1)
-
-
-def unpack(slots, og, kv):
-    def spec(which):
-        return pl.BlockSpec((3, 1, 2, BLOCK, 128), lambda i, slots: (0, slots[2 * i + which], 0, 0, 0))
-
+def unpack_kernel(og_src, kv_src, o_out, dq_out, dk_out, dv_out, og, kv, o_ref, dq_ref, dk_ref, dv_ref, in_sem, out_sem):
+    me = lax.axis_index("seq")
+    z, x = me // 4, me % 4
+    loads = []
+    for g in range(PEERS):
+        slot = slot_of(g // 4 - z + 4, g % 4 - x + 4)
+        pair = [
+            pltpu.make_async_copy(src.at[:, slot], dst.at[g], in_sem.at[i, g])
+            for i, (src, dst) in enumerate(((og_src, og), (kv_src, kv)))
+        ]
+        for load in pair:
+            load.start()
+        loads.append(pair)
+    left = lax.broadcasted_iota(jnp.int32, (BLOCK, 128), 1) < HDIM
+    stores = []
+    for i in range(PEERS // 2):
+        for g in (2 * i, 2 * i + 1):
+            for load in loads[g]:
+                load.wait()
+        for t in range(3):
+            cols = slice(384 * i + 128 * t, 384 * i + 128 * t + 128)
+            a, b = 6 * i + 2 * t, 6 * i + 2 * t + 1
+            for part in range(2):
+                rows = slice(BLOCK * part, BLOCK * part + BLOCK)
+                for src, low, high in ((og, dq_ref, o_ref), (kv, dk_ref, dv_ref)):
+                    one, two = src[a // 3, a % 3, part], src[b // 3, b % 3, part]
+                    low[rows, cols] = jnp.where(left, one, pltpu.roll(two, HDIM, 1))
+                    high[rows, cols] = jnp.where(left, pltpu.roll(one, HDIM, 1), two)
+        cols = slice(384 * i, 384 * i + 384)
+        for n, (src, dst) in enumerate(((o_ref, o_out), (dq_ref, dq_out), (dk_ref, dk_out), (dv_ref, dv_out))):
+            store = pltpu.make_async_copy(src.at[:, cols], dst.at[:, cols], out_sem.at[n, i])
+            store.start()
+            stores.append(store)
+    for store in stores:
+        store.wait()
+
+
+def unpack(og, kv):
     rows = 2 * BLOCK
-    out_spec = pl.BlockSpec((rows, 384), lambda i, slots: (0, i))
+    any_spec = pl.BlockSpec(memory_space=pl.ANY)
     out = jax.ShapeDtypeStruct((rows, 3072), og.dtype)
     return pl.pallas_call(
         unpack_kernel,
-        grid_spec=pltpu.PrefetchScalarGridSpec(
-            num_scalar_prefetch=1,
-            grid=(8,),
-            in_specs=[spec(0), spec(1), spec(0), spec(1)],
-            out_specs=[out_spec] * 4,
-        ),
+        in_specs=[any_spec] * 2,
+        out_specs=[any_spec] * 4,
         out_shape=[out] * 4,
-        cost_estimate=pl.CostEstimate(flops=0, bytes_accessed=12 << 20, transcendentals=0),
+        scratch_shapes=[pltpu.VMEM((PEERS, 3, 2, BLOCK, 128), og.dtype)] * 2
+        + [pltpu.VMEM((rows, 3072), og.dtype)] * 4
+        + [pltpu.SemaphoreType.DMA((2, PEERS)), pltpu.SemaphoreType.DMA((4, PEERS // 2))],
         name="unpack",
-    )(slots, og, og, kv, kv)
+    )(og, kv)
 
 
 def nt(a, b):
@@ -79,6 +96,9 @@
         source = block >> 1
         rel = ((((source >> 2) - z) & 3) << 2) + (((source & 3) - x) & 3)
         return (((rel * STEP) & (PEERS - 1)) << 1) + (block & 1)
+
+    def turn(ids):
+        return jnp.where(ids < blocks, ids + 2 * CROSS, ids - blocks)
 
     rows = []
     hits = [jnp.zeros((1, 128), i32), jnp.zeros((1, 128), i32)]
@@ -114,7 +134,7 @@
         ids = jnp.where(
             row < 0, blocks + outside[0], jnp.where(row < blocks, place(row), blocks + CROSS + outside[1])
         )
-        key = ids * entries + number
+        key = turn(ids) * entries + number
         rank = total(turned(key, entries) < key, 1)
         column, rank = turned(ids, entries), turned(rank, entries)
         lands = rank == order
@@ -123,17 +143,17 @@
         tab_ref[h, 0:1] = ids
         tab_ref[h, 1:2] = total(lands, grid(entries, entries, 0))
         tab_ref[h, 2:3] = jnp.where((ranked == ahead) & (number > 0), 1, 0)
-        upto = total(column <= order, 1)
+        upto = total(turn(column) <= turn(order), 1)
         held = total(column == order, 1)
         tab_ref[h, 3:4] = jnp.where(held > 0, upto - 1, entries)
 
 
 def fused_kernel(
-    pat_ref, q_src, k_src, v_src, g_src, og_out, dkv_out,
-    raw_q, raw_k, raw_v, raw_g, tabv, tab, askv, gotv, got,
+    pat_src, q_src, k_src, v_src, g_src, og_out, dkv_out,
+    pat_ref, raw_q, raw_k, raw_v, raw_g, tabv, tab, askv, gotv, got,
     kvin, qgin, kvx, stage, kvw, kvt, terms, seg, ogs, dks, sums, back, near, sd0, sd1, ex0, ex1,
     in_send, in_recv, in_self, x_send, x_recv, b_send, b_recv, o_send, o_recv, o_self,
-    raw_sem, tab_sem, got_sem, a_send, a_recv,
+    raw_sem, pat_sem, tab_sem, got_sem, a_send, a_recv, q_recv,
     *, heads, blocks, per_list,
 ):
     bf16, f32 = jnp.bfloat16, jnp.float32
@@ -156,6 +176,8 @@
     loads = [pltpu.make_async_copy(src, dst, raw_sem.at[i]) for i, (src, dst) in enumerate(raws)]
     for load in loads:
         load.start()
+    pattern = pltpu.make_async_copy(pat_src, pat_ref, pat_sem.at[0])
+    pattern.start()
     barrier = pltpu.get_barrier_semaphore()
     for dz, dx in SPREAD:
         pl.semaphore_signal(barrier, 1, device_id={"seq": peer(dz, dx)}, device_id_type=MESH)
@@ -163,7 +185,7 @@
         pl.semaphore_signal(barrier, 1, device_id=device, device_id_type=MESH)
     pl.semaphore_wait(barrier, len(SPREAD) + 2)
 
-    inputs = ((raw_k, raw_v, dks, kvin), (raw_q, raw_g, ogs, qgin))
+    inputs = ((raw_k, raw_v, ogs, kvin), (raw_q, raw_g, dks, qgin))
 
     def input_self(t, h):
         return pltpu.make_async_copy(
@@ -173,9 +195,11 @@
     def send_input(t, h, p):
         rel = p * STEP % PEERS
         dz, dx = rel // 4, rel % 4
-        there = inputs[t][3].at[h, pl.ds(2 * slot_of(4 - dz, 4 - dx), 2)]
+        slot = slot_of(4 - dz, 4 - dx)
+        there = inputs[t][3].at[h, pl.ds(2 * slot, 2)]
         src = inputs[t][2].at[h, pl.ds(2 * p, 2)]
-        remote(src, there, in_send.at[t, h], in_recv.at[t, h], {"seq": peer(dz, dx)}).start()
+        landing = in_recv.at[h] if t == 0 else q_recv.at[h, slot]
+        remote(src, there, in_send.at[t, h], landing, {"seq": peer(dz, dx)}).start()
 
     for h in range(heads):
         for t in range(2):
@@ -212,15 +236,16 @@
 
             send_input(t, h, PEERS - 1)
 
-    def arrived(t, h):
-        input_self(t, h).wait()
-        rest = inputs[t][3].at[h, pl.ds(2, blocks - 2)]
-        pltpu.make_async_copy(rest, rest, in_recv.at[t, h]).wait()
+    def arrived(h):
+        input_self(0, h).wait()
+        rest = kvin.at[h, pl.ds(2, blocks - 2)]
+        pltpu.make_async_copy(rest, rest, in_recv.at[h]).wait()
 
     def sent(t, h):
         rest = inputs[t][2].at[h, pl.ds(2, blocks - 2)]
         pltpu.make_async_copy(rest, rest, in_send.at[t, h]).wait()
 
+    pattern.wait()
     plan(pat_ref, tabv, askv, slab * blocks, z, x, heads, blocks, per_list)
     asking = [remote(askv.at[i], gotv.at[i], a_send.at[i], a_recv.at[i], (before, after)[i]) for i in range(2)]
     for ask in asking:
@@ -247,7 +272,7 @@
         )
 
     def open_window(h):
-        arrived(0, h)
+        arrived(h)
 
         @pl.loop(0, blocks)
         def _(w):
@@ -285,12 +310,19 @@
             block = kvx[h, c]
             kvw[blocks + c] = block
             kvt[blocks + c] = block.T
-        arrived(1, h)
         sent(0, h)
-        sent(1, h)
 
         @pl.loop(0, blocks // 2)
         def _(p):
+            @pl.when(p == 0)
+            def _():
+                input_self(1, h).wait()
+
+            @pl.when(p > 0)
+            def _():
+                chunk = qgin.at[h, pl.ds(2 * p, 2)]
+                pltpu.make_async_copy(chunk, chunk, q_recv.at[h, p]).wait()
+
             @pl.when(p == 1)
             def _():
                 output_self(ogs, og_out, 0, h).start()
@@ -353,28 +385,37 @@
             seg[t] = acc.astype(bf16)
             return acc
 
-        lax.fori_loop(0, entries, running, jnp.zeros((BLOCK, 128), f32))
+        acc = lax.fori_loop(0, entries // 2, running, jnp.zeros((BLOCK, 128), f32))
         for c in range(2 * CROSS):
             sums[h, c] = seg[tab[h, 3, blocks + c]]
+        acc = lax.fori_loop(entries // 2, entries // 2 + 8, running, acc)
         for side in range(2):
             returning(h, side).start()
+        lax.fori_loop(entries // 2 + 8, entries, running, acc)
+        sent(1, h)
         for side in range(2):
             returning(h, side).wait_recv()
         for c in range(2 * CROSS):
             near[c] = back[h, c]
 
-        @pl.loop(0, blocks)
-        def _(w):
-            total = seg[tab[h, 3, w]].astype(f32)
-            total += near[got[0, 1, w]].astype(f32)
-            total += near[got[1, 1, w]].astype(f32)
-            dks[h, w] = total.astype(bf16)
-
-        output_self(dks, dkv_out, 1, h).start()
-
-        @pl.loop(1, blocks // 2)
+        @pl.loop(0, blocks // 2)
         def _(p):
-            output(dks, dkv_out, 1, h, p).start()
+            for half in range(2):
+                w = 2 * p + half
+                total = seg[tab[h, 3, w]].astype(f32)
+                total += near[got[0, 1, w]].astype(f32)
+                total += near[got[1, 1, w]].astype(f32)
+                dks[h, w] = total.astype(bf16)
+
+            @pl.when(p == 1)
+            def _():
+                output_self(dks, dkv_out, 1, h).start()
+
+            @pl.when(p > 1)
+            def _():
+                output(dks, dkv_out, 1, h, p - 1).start()
+
+        output(dks, dkv_out, 1, h, blocks // 2 - 1).start()
 
     for h in range(heads):
         for side in range(2):
@@ -399,10 +440,11 @@
     any_spec = pl.BlockSpec(memory_space=pl.ANY)
     return pl.pallas_call(
         functools.partial(fused_kernel, heads=heads, blocks=blocks, per_list=per_list),
-        in_specs=[pl.BlockSpec(memory_space=pltpu.VMEM)] + [any_spec] * 4,
+        in_specs=[any_spec] * 5,
         out_specs=[any_spec, any_spec],
         out_shape=[out, out],
-        scratch_shapes=[pltpu.VMEM(q.shape, bf16)] * 4
+        scratch_shapes=[pltpu.VMEM(pattern.shape, jnp.int32)]
+        + [pltpu.VMEM(q.shape, bf16)] * 4
         + [
             pltpu.VMEM((heads, 8, entries), jnp.int32),
             pltpu.SMEM((heads, 8, entries), jnp.int32),
@@ -427,10 +469,10 @@
             pltpu.VMEM((per_list, BLOCK, 2 * BLOCK), bf16),
             pltpu.VMEM((per_list, BLOCK, 2 * BLOCK), bf16),
         ]
-        + [sems((2, heads))] * 3
+        + [sems((2, heads)), sems((heads,)), sems((2, heads))]
         + [sems((heads, 2))] * 4
         + [sems((2, heads))] * 3
-        + [sems((4,)), sems((1,)), sems((1,)), sems((2,)), sems((2,))],
+        + [sems((4,)), sems((1,)), sems((1,)), sems((1,)), sems((2,)), sems((2,)), sems((heads, PEERS))],
         compiler_params=pltpu.CompilerParams(
             collective_id=0, has_side_effects=True, vmem_limit_bytes=60 << 20
         ),
@@ -439,11 +481,8 @@
 
 
 def local(query, key, value, d_out, pattern):
-    me = lax.axis_index("seq")
-    z, x = me // 4, me % 4
     og, dkv = fused(pattern, query, key, value, d_out)
-    group = jnp.arange(PEERS, dtype=jnp.int32)
-    return tuple(unpack(slot_of(group // 4 - z + 4, group % 4 - x + 4), og, dkv))
+    return tuple(unpack(og, dkv))
 
 
 def solution(mesh):

time: 167 us -> 155 us (0.928)
  Pallas kernels: 164 us -> 153 us
    pallas_call x1, Pallas kernels: 154 us -> 147 us  [fused(): pl.pallas_call(functools.partial(fused_kernel, heads=heads, blocks=blocks...]
    pallas_call x1, Pallas kernels: 9.47 us -> 5.79 us  [unpack(): pl.pallas_call(unpack_kernel, in_specs=[any_spec] * 2, out_specs=[any_spe...]
where the time goes in v3:
time: 155 us
  Pallas kernels  153 us (99%)
    pallas_call x1, Pallas kernels, fused(): pl.pallas_call(functools.partial(fused_kernel, heads=heads, blocks=blocks...  147 us
    pallas_call x1, Pallas kernels, unpack(): pl.pallas_call(unpack_kernel, in_specs=[any_spec] * 2, out_specs=[any_spe...  5.79 us

profile of v3, /device:TPU:0, one launch (start us, length us, event | category | flops | bytes accessed | tf_op | source)
XLA Modules:
  0.0 154.6 jit_solution(18003141501429862661)
XLA Ops:
  0.6 1.4 copy.9.pat_src
  2.0 146.7 %fused.1 = (bf16[3,16,2,128,128]{4,3,2,1,0:T(8,128)(2,1)}, bf16[3,16,2,128,128]{4,3,2,1,0:T(8,128)(2,1)}) custom-call(s32[3,32,8]{2,1,0:T(8,128)} %copy.9.pat_src, bf16[256,3072]{1,0:T(8,128)(2,1)} %q_src.1, bf16[256,3072]{1,0:T(8,128)(2,1)} %k_src.1, bf16[256,3072]{1,0:T(8,128)(2,1)} %v_src.1, bf16[256,3072]{1,0:T(8,128)(2,1)} %g_src.1), custom_call_target="tpu_custom_call" | custom-call | tf_op jit(solution)/shard_map/fused/pallas_call | solution.py:441
  148.8 5.8 %unpack.1 = (bf16[256,3072]{1,0:T(8,128)(2,1)}, bf16[256,3072]{1,0:T(8,128)(2,1)}, bf16[256,3072]{1,0:T(8,128)(2,1)}, bf16[256,3072]{1,0:T(8,128)(2,1)}) custom-call(bf16[3,16,2,128,128]{4,3,2,1,0:T(8,128)(2,1)} %get-tuple-element.6.og_src, bf16[3,16,2,128,128]{4,3,2,1,0:T(8,128)(2,1)} %get-tuple-element.7.kv_src), custom_call_target="tpu_custom_call" | custom-call | tf_op jit(solution)/shard_map/unpack/pallas_call | solution.py:65

commit v4 on v3

--- a/solution.py
+++ b/solution.py
@@ -105,12 +105,8 @@
     spot = grid(entries, 128, 1)
     for h in range(heads):
         pattern = pat_ref[h]
-        lane = grid(blocks, entries, 1)
-        spread = jnp.zeros((blocks, entries), i32)
-        for j in range(per_list):
-            spread = jnp.where((lane & (per_list - 1)) == j, pattern[:, j : j + 1], spread)
-        mine = (lane >> 3) == grid(blocks, entries, 0)
-        rows.append(total(mine, spread) - base)
+        mine = grid(per_list, entries, 1) // blocks == grid(per_list, entries, 0)
+        rows.append(total(mine, jnp.concatenate([pattern] * per_list, axis=1)) - base)
         column = turned(rows[h], entries)[:, :128]
         for side, shift in enumerate((-blocks, blocks)):
             found = (column == spot + shift) & (spot < blocks)
@@ -332,15 +328,15 @@
                 output(ogs, og_out, 0, h, p - 1).start()
 
             rel = p * STEP % PEERS
-            first = 2 * per_list * peer(rel // 4, rel % 4)
+            first = 2 * peer(rel // 4, rel % 4)
             pairs = []
             for half, (sd, ex) in enumerate(((sd0, ex0), (sd1, ex1))):
                 b = 2 * p + half
                 qg = qgin[h, b]
                 zero = jnp.zeros_like(qg)
                 both = jnp.concatenate([jnp.where(left, qg, zero), jnp.where(left, zero, qg)], axis=0)
-                base = first + half * per_list
-                ids = [tab[h, 0, base + j] for j in range(per_list)]
+                base = first + half
+                ids = [tab[h, 0, base + j * blocks] for j in range(per_list)]
                 top = None
                 for j in range(per_list):
                     pair = nt(kvw[ids[j]], both)
@@ -371,7 +367,7 @@
                 column = jnp.broadcast_to(inverse, (BLOCK, BLOCK)).T
                 scaled = (both.astype(f32) * jnp.concatenate([column, column], axis=0)).astype(bf16)
                 for j in range(per_list):
-                    terms[base + j] = jnp.dot(ex[j], scaled, preferred_element_type=f32)
+                    terms[base + j * blocks] = jnp.dot(ex[j], scaled, preferred_element_type=f32)
 
         @pl.when(h + 1 < heads)
         def _():
@@ -430,7 +426,7 @@
 
 
 def fused(pattern, q, k, v, g):
-    heads, blocks, per_list = pattern.shape
+    heads, per_list, blocks = pattern.shape
     f32, bf16 = jnp.float32, jnp.bfloat16
     window = blocks + 2 * CROSS
     entries = blocks * per_list
@@ -481,7 +477,7 @@
 
 
 def local(query, key, value, d_out, pattern):
-    og, dkv = fused(pattern, query, key, value, d_out)
+    og, dkv = fused(jnp.transpose(pattern, (0, 2, 1)), query, key, value, d_out)
     return tuple(unpack(og, dkv))
 
 

time: 155 us -> 154 us (level)
  no operation moved by 1% of the time
where the time goes in v4:
time: 154 us; the launch traced here: 153 us
  Pallas kernels  153 us (99%)
    pallas_call x1, Pallas kernels, fused(): pl.pallas_call(functools.partial(fused_kernel, heads=heads, blocks=blocks...  147 us
    pallas_call x1, Pallas kernels, unpack(): pl.pallas_call(unpack_kernel, in_specs=[any_spec] * 2, out_specs=[any_spe...  5.79 us

profile of v4, /device:TPU:0, one launch (start us, length us, event | category | flops | bytes accessed | tf_op | source)
XLA Modules:
  0.0 153.3 jit_solution(13861587756756230378)
XLA Ops:
  0.6 146.9 %fused.1 = (bf16[3,16,2,128,128]{4,3,2,1,0:T(8,128)(2,1)}, bf16[3,16,2,128,128]{4,3,2,1,0:T(8,128)(2,1)}) custom-call(s32[3,8,32]{2,1,0:T(8,128)} %bitcast.1, bf16[256,3072]{1,0:T(8,128)(2,1)} %q_src.1, bf16[256,3072]{1,0:T(8,128)(2,1)} %k_src.1, bf16[256,3072]{1,0:T(8,128)(2,1)} %v_src.1, bf16[256,3072]{1,0:T(8,128)(2,1)} %g_src.1), custom_call_target="tpu_custom_call" | custom-call | tf_op jit(solution)/shard_map/fused/pallas_call | solution.py:437
  147.5 5.8 %unpack.1 = (bf16[256,3072]{1,0:T(8,128)(2,1)}, bf16[256,3072]{1,0:T(8,128)(2,1)}, bf16[256,3072]{1,0:T(8,128)(2,1)}, bf16[256,3072]{1,0:T(8,128)(2,1)}) custom-call(bf16[3,16,2,128,128]{4,3,2,1,0:T(8,128)(2,1)} %get-tuple-element.6.og_src, bf16[3,16,2,128,128]{4,3,2,1,0:T(8,128)(2,1)} %get-tuple-element.7.kv_src), custom_call_target="tpu_custom_call" | custom-call | tf_op jit(solution)/shard_map/unpack/pallas_call | solution.py:65

commit v5 on v4

--- a/solution.py
+++ b/solution.py
@@ -350,24 +350,23 @@
                 for j in range(per_list):
                     e = jnp.exp(sd[j, :, :BLOCK] - row_max)
                     sd[j, :, :BLOCK] = e
-                    ex[j, :, BLOCK:] = e.astype(bf16)
                     total += jnp.sum(e.reshape(16, 8, BLOCK), axis=0)
                     mixed += jnp.sum((e * sd[j, :, BLOCK:]).reshape(16, 8, BLOCK), axis=0)
                 inverse = 1.0 / jnp.sum(total, axis=0, keepdims=True)
                 correction = jnp.sum(mixed, axis=0, keepdims=True) * inverse
                 for j in range(per_list):
-                    ex[j, :, :BLOCK] = (sd[j, :, :BLOCK] * (sd[j, :, BLOCK:] - correction)).astype(bf16)
+                    weights = sd[j, :, :BLOCK] * inverse
+                    ex[j, :, BLOCK:] = weights.astype(bf16)
+                    ex[j, :, :BLOCK] = (weights * (sd[j, :, BLOCK:] - correction)).astype(bf16)
                 out = jnp.zeros((128, 2 * BLOCK), f32)
                 for j in range(0, per_list, 2):
                     lhs = jnp.concatenate([kvt[ids[j]], kvt[ids[j + 1]]], axis=1)
                     rhs = ex[j : j + 2].reshape(2 * BLOCK, 2 * BLOCK)
                     out += jnp.dot(lhs, rhs, preferred_element_type=f32)
-                outs = jnp.concatenate([out[:HDIM, :BLOCK] * (inverse * SCALE), out[HDIM:, BLOCK:] * inverse], axis=0)
+                outs = jnp.concatenate([out[:HDIM, :BLOCK] * SCALE, out[HDIM:, BLOCK:]], axis=0)
                 ogs[h, b] = outs.T.astype(bf16)
-                column = jnp.broadcast_to(inverse, (BLOCK, BLOCK)).T
-                scaled = (both.astype(f32) * jnp.concatenate([column, column], axis=0)).astype(bf16)
                 for j in range(per_list):
-                    terms[base + j * blocks] = jnp.dot(ex[j], scaled, preferred_element_type=f32)
+                    terms[base + j * blocks] = jnp.dot(ex[j], both, preferred_element_type=f32)
 
         @pl.when(h + 1 < heads)
         def _():

time: 154 us -> 154 us (level)
  no operation moved by 1% of the time
where the time goes in v5:
time: 154 us; the launch traced here: 153 us
  Pallas kernels  153 us (99%)
    pallas_call x1, Pallas kernels, fused(): pl.pallas_call(functools.partial(fused_kernel, heads=heads, blocks=blocks...  147 us
    pallas_call x1, Pallas kernels, unpack(): pl.pallas_call(unpack_kernel, in_specs=[any_spec] * 2, out_specs=[any_spe...  5.79 us

profile of v5, /device:TPU:0, one launch (start us, length us, event | category | flops | bytes accessed | tf_op | source)
XLA Modules:
  0.0 153.3 jit_solution(1902063091262752045)
XLA Ops:
  0.6 146.9 %fused.1 = (bf16[3,16,2,128,128]{4,3,2,1,0:T(8,128)(2,1)}, bf16[3,16,2,128,128]{4,3,2,1,0:T(8,128)(2,1)}) custom-call(s32[3,8,32]{2,1,0:T(8,128)} %bitcast.1, bf16[256,3072]{1,0:T(8,128)(2,1)} %q_src.1, bf16[256,3072]{1,0:T(8,128)(2,1)} %k_src.1, bf16[256,3072]{1,0:T(8,128)(2,1)} %v_src.1, bf16[256,3072]{1,0:T(8,128)(2,1)} %g_src.1), custom_call_target="tpu_custom_call" | custom-call | tf_op jit(solution)/shard_map/fused/pallas_call | solution.py:436
  147.6 5.8 %unpack.1 = (bf16[256,3072]{1,0:T(8,128)(2,1)}, bf16[256,3072]{1,0:T(8,128)(2,1)}, bf16[256,3072]{1,0:T(8,128)(2,1)}, bf16[256,3072]{1,0:T(8,128)(2,1)}) custom-call(bf16[3,16,2,128,128]{4,3,2,1,0:T(8,128)(2,1)} %get-tuple-element.6.og_src, bf16[3,16,2,128,128]{4,3,2,1,0:T(8,128)(2,1)} %get-tuple-element.7.kv_src), custom_call_target="tpu_custom_call" | custom-call | tf_op jit(solution)/shard_map/unpack/pallas_call | solution.py:65
